TPU v7x, 32 devices: a whole 2x2x4 slice. The times are simulated.
32 devices in a mesh: strip: 2 (over x), az: 4 (over z), tile: 4 (over y, core).
Axes of the slice: x: 2, y: 2, z: 4, core: 2. Of those that a mesh axis runs over, the one named last changes fastest.
Arguments:
- raw_echo: float32 [2, 4096, 4096], P(None, ('strip', 'az', 'tile')), parts along dimension 1, may hold values from -6 to 6
- phase_scaling: float32 [1024, 4096], P(None, 'tile'), may hold values from -3.140625 to 3.140625
- phase_range: float32 [1024, 4096], P('tile'), may hold values from -3.140625 to 3.140625
- phase_azimuth: float32 [1024, 4096], P(None, 'tile'), may hold values from -3.140625 to 3.140625
Outputs:
- image: float32 [2, 4096, 4096], P(None, ('strip', 'az'), 'tile'), parts along dimension 1
There are 2 independent parts, one for each index of `strip`. A program takes and returns all parts, laid end to end along the dimension named above; an argument that names none is the same for every part. Nothing has to cross between parts.
All inputs are finite; a program needn't handle non-finite values.
Results may differ from a plain program's by a relative error of at most 0.00007.
Values sent between devices are 32-bit elements; how exact they have to be, the bound alone decides.
A program may use at most 128 MiB of HBM per device.

v0:
```python
import math

import jax
import jax.numpy as jnp
from jax import lax
from jax.sharding import PartitionSpec as P


def from_behind(value, axis, by):
    length = lax.axis_size(axis)
    pairs = [(i, i + by) for i in range(length) if 0 <= i + by < length]
    return lax.ppermute(value, axis, pairs)


def split_length(extent):
    return (extent // 128, 128)


def unit_roots(row_lo, row_hi, col_count, modulus, direction):
    row_index = jnp.arange(row_lo, row_hi, dtype=jnp.int32)
    col_index = jnp.arange(col_count, dtype=jnp.int32)
    residue = row_index[:, None] * col_index[None, :] % modulus
    phase_angle = residue.astype(jnp.float32) * (direction * 2.0 * math.pi / modulus)
    return (jnp.cos(phase_angle), jnp.sin(phase_angle))


def complex_mix(spec, table, values):

    def mixing(left, right):
        return jnp.einsum(spec, left, right, precision=lax.Precision.HIGHEST)

    return (
        mixing(table[0], values[0]) - mixing(table[1], values[1]),
        mixing(table[0], values[1]) + mixing(table[1], values[0]),
    )


def rotate(values, table):
    return (
        values[0] * table[0] - values[1] * table[1],
        values[0] * table[1] + values[1] * table[0],
    )


def azimuth_front(values, direction):
    extent, width = values[0].shape
    n_one, n_two = split_length(extent)
    shaped = (values[0].reshape(n_one, n_two, width), values[1].reshape(n_one, n_two, width))
    sectioned = complex_mix("ka,abc->kbc", unit_roots(0, n_one, n_one, n_one, direction), shaped)
    twist = unit_roots(0, n_one, n_two, extent, direction)
    return rotate(sectioned, (twist[0][:, :, None], twist[1][:, :, None]))


def azimuth_back(sectioned, direction, row_lo, row_hi):
    n_one, n_two, width = sectioned[0].shape
    table = unit_roots(row_lo, row_hi, n_two, n_two, direction)
    mixed = complex_mix("mb,kbc->mkc", table, sectioned)
    row_count = (row_hi - row_lo) * n_one
    return (mixed[0].reshape(row_count, width), mixed[1].reshape(row_count, width))


def range_forward(values):
    width, extent = values[0].shape
    n_one, n_two = split_length(extent)
    shaped = (values[0].reshape(width, n_one, n_two), values[1].reshape(width, n_one, n_two))
    sectioned = complex_mix("ka,cab->ckb", unit_roots(0, n_one, n_one, n_one, -1.0), shaped)
    sectioned = rotate(sectioned, unit_roots(0, n_one, n_two, extent, -1.0))
    mixed = complex_mix("mb,ckb->ckm", unit_roots(0, n_two, n_two, n_two, -1.0), sectioned)
    return (mixed[0].reshape(width, extent), mixed[1].reshape(width, extent))


def range_inverse(values):
    width, extent = values[0].shape
    n_one, n_two = split_length(extent)
    shaped = (values[0].reshape(width, n_one, n_two), values[1].reshape(width, n_one, n_two))
    sectioned = complex_mix("mb,ckm->ckb", unit_roots(0, n_two, n_two, n_two, 1.0), shaped)
    sectioned = rotate(sectioned, unit_roots(0, n_one, n_two, extent, 1.0))
    mixed = complex_mix("ka,ckb->cab", unit_roots(0, n_one, n_one, n_one, 1.0), sectioned)
    scale = 1.0 / extent
    return (mixed[0].reshape(width, extent) * scale, mixed[1].reshape(width, extent) * scale)


def body(raw_echo, phase_scaling, phase_range, phase_azimuth):
    tile_count = lax.axis_size("tile")
    columns = lax.all_to_all(raw_echo, "tile", split_axis=2, concat_axis=1, tiled=True)
    pulse_count = columns.shape[1]
    width = columns.shape[2]
    extent = phase_scaling.shape[0]
    tail_count = extent - pulse_count
    padded = jnp.pad(columns, ((0, 0), (0, tail_count), (0, 0)))
    forward = azimuth_front((padded[0], padded[1]), -1.0)
    spectrum = azimuth_back(forward, -1.0, 0, forward[0].shape[1])
    spectrum = rotate(spectrum, (jnp.cos(phase_scaling), jnp.sin(phase_scaling)))
    grouped = jnp.stack(spectrum).reshape(2, tile_count, extent // tile_count, width)
    doppler = lax.all_to_all(grouped, "tile", split_axis=1, concat_axis=3, tiled=True)
    row_count = doppler.shape[2]
    range_count = doppler.shape[3]
    r_one, r_two = split_length(range_count)
    spectral = range_forward((doppler[0, 0], doppler[1, 0]))
    permuted = (
        phase_range.reshape(row_count, r_two, r_one)
        .transpose(0, 2, 1)
        .reshape(row_count, range_count)
    )
    spectral = rotate(spectral, (jnp.cos(permuted), jnp.sin(permuted)))
    filtered = range_inverse(spectral)
    returned = lax.all_to_all(
        jnp.stack(filtered)[:, None], "tile", split_axis=3, concat_axis=1, tiled=True
    )
    returned = returned.reshape(2, extent, width)
    compressed = rotate(
        (returned[0], returned[1]), (jnp.cos(phase_azimuth), jnp.sin(phase_azimuth))
    )
    sectioned = azimuth_front(compressed, 1.0)
    a_one = sectioned[0].shape[0]
    a_two = sectioned[0].shape[1]
    scale = 1.0 / extent
    tail_lo = pulse_count // a_one
    head_hi = -(-pulse_count // a_one)
    tail_part = azimuth_back(sectioned, 1.0, tail_lo, a_two)
    offset = pulse_count - tail_lo * a_one
    tail_block = jnp.stack(tail_part) * scale
    incoming = from_behind(tail_block, "az", 1)
    head_part = azimuth_back(sectioned, 1.0, 0, head_hi)
    head_block = jnp.stack(head_part) * scale
    return jnp.concatenate([head_block + incoming, head_block[:, tail_count:]], axis=1)


def solution(mesh):
    return jax.shard_map(
        body,
        mesh=mesh,
        in_specs=(
            P(None, ("strip", "az", "tile"), None),
            P(None, "tile"),
            P("tile", None),
            P(None, "tile"),
        ),
        out_specs=P(None, ("strip", "az"), "tile"),
        check_vma=False,
    )
```

profile of v0, /device:TPU:0, one launch (start us, length us, event | category | flops | bytes accessed | tf_op | source)
XLA Modules:
  0.0 706.1 jit_solution(165255690241581472)
XLA Ops:
  0.0 7.2 %copy.181 = f32[2,128,4096]{1,0,2:T(2,128)} copy(f32[2,128,4096]{2,1,0:T(8,128)} %param.4) | data formatting | bytes 8388608 | tf_op args[0]
  7.2 4.9 all-to-all-start
  12.4 16.6 %fusion.398 = (f32[1024,1024]{1,0:T(8,128)}, f32[1024,1024]{1,0:T(8,128)}) fusion(f32[1024,1024]{1,0:T(8,128)} %param.5), kind=kLoop, calls=%fused_computation.414 | loop fusion | bytes 12582912 | tf_op jit(solution)/shard_map/sin | solution.py:93
  29.0 32.0 %all-to-all-done = f32[2,128,4096]{1,0,2:T(2,128)} async-done(((f32[2,128,4096]{1,0,2:T(2,128)}), f32[2,128,4096]{1,0,2:T(2,128)}, u32[]{:S(2)}, u32[]{:S(2)}) %all-to-all-start) | async-done | bytes 4194336 | tf_op jit(solution)/shard_map/all_to_all | solution.py:85
  61.1 4.4 copy.182
  65.5 5.4 copy.183
  74.2 6.3 fusion.43
  80.5 6.6 fusion.41
  87.2 6.3 fusion.65
  93.5 7.4 %multiply_subtract_fusion.2 = (f32[8,128,1024]{2,0,1:T(8,128)S(1)}, f32[8,128,1024]{2,0,1:T(8,128)S(1)}) fusion(f32[8,128,1024]{2,0,1:T(8,128)S(1)} %fusion.65, f32[8,128]{0,1:T(8,128)S(1)} %copy.189, f32[8,128]{0,1:T(8,128)S(1)} %copy.186, f32[8,128,1024]{2,0,1:T(8,128)S(1)} %fusion.41, f32[8,128,1024]{2,1,0:T(8,128)S(1)} %bitcast.205), kind=kOutput, calls=%fused_computation.38 | convolution fusion | flops 108004224 | bytes 20979712 | tf_op jit(solution)/shard_map/ka,abc->kbc/dot_general | solution.py:30
  100.8 6.0 fusion.35
  106.9 6.4 fusion.33
  113.3 6.3 fusion.71
  119.7 6.5 fusion.74
  126.2 9.6 %fusion.7 = (f32[1024,1024]{1,0:T(8,128)S(1)}, f32[1024,1024]{1,0:T(8,128)S(1)}) fusion(f32[1024,1024]{1,0:T(8,128)S(1)} %copy-done.7, f32[1024,1024]{1,0:T(8,128)S(1)} %copy-done.8, f32[128,8,1024]{2,0,1:T(8,128)S(1)} %fusion.74, f32[128,8,1024]{2,0,1:T(8,128)S(1)} %fusion.71), kind=kLoop, calls=%fused_computation.27 | loop fusion | flops 6291456 | bytes 25165824 | tf_op jit(solution)/shard_map/sub | solution.py:40
  140.1 5.6 all-to-all-start.1
  145.8 5.6 copy.206
  151.4 16.6 %fusion.397 = (f32[256,4096]{0,1:T(8,128)}, f32[256,4096]{0,1:T(8,128)}) fusion(f32[256,4096]{0,1:T(8,128)} %copy.206), kind=kLoop, calls=%fused_computation.413 | loop fusion | bytes 12582912 | tf_op jit(solution)/shard_map/cos | solution.py:105
  168.0 5.3 copy.207
  173.3 5.3 copy.211
  178.8 60.2 %all-to-all-done.1 = f32[2,4,256,1024]{3,2,0,1:T(8,128)} async-done(((f32[2,4,256,1024]{3,2,0,1:T(8,128)}), f32[2,4,256,1024]{3,2,0,1:T(8,128)}, u32[]{:S(2)}, u32[]{:S(2)}) %all-to-all-start.1) | async-done | bytes 8388640 | tf_op jit(solution)/shard_map/all_to_all | solution.py:95
  238.9 6.7 fusion.395
  245.7 4.7 copy.198
  250.4 5.6 reshape_squeeze.14
  256.0 8.1 %fusion.180 = f32[256,128,32]{1,2,0:T(8,128)} fusion(f32[256,32,128]{2,1,0:T(8,128)} %reshape_squeeze.14), kind=kOutput, calls=%fused_computation.197 | convolution fusion | flops 402667520 | bytes 8388608 | tf_op jit(solution)/shard_map/ka,cab->ckb/dot_general | solution.py:30
  264.1 4.7 copy.200
  268.8 5.5 reshape_squeeze.15
  274.3 6.3 fusion.178
  284.7 4.7 fusion.5
  289.3 6.9 fusion.27
  296.3 8.7 %fusion.25 = f32[256,32,128]{2,0,1:T(8,128)} fusion(f32[256,32,128]{2,1,0:T(8,128)S(1)} %get-tuple-element.18), kind=kOutput, calls=%fused_computation.55 | convolution fusion | flops 1610842112 | bytes 8388608 | tf_op jit(solution)/shard_map/mb,ckb->ckm/dot_general | solution.py:30
  305.0 6.9 fusion.77
  311.9 9.6 %fusion.3 = (f32[256,32,128]{2,0,1:T(8,128)S(1)}, f32[256,32,128]{2,0,1:T(8,128)S(1)}) fusion(f32[256,128,32]{1,0,2:T(8,128)S(1)} %copy-done.5, f32[256,32,128]{2,0,1:T(8,128)S(1)} %fusion.77, f32[256,128,32]{1,0,2:T(8,128)S(1)} %copy-done.4, f32[256,32,128]{2,0,1:T(8,128)} %fusion.25, f32[256,32,128]{2,1,0:T(8,128)S(1)} %get-tuple-element.17), kind=kOutput, calls=%fused_computation.15 | convolution fusion | flops 1618182144 | bytes 29360128 | tf_op jit(solution)/shard_map/mb,ckb->ckm/dot_general | solution.py:30
  332.5 4.7 multiply_subtract_fusion.1
  337.2 6.3 fusion.19
  343.6 9.1 %fusion.17 = f32[256,128,32]{1,2,0:T(8,128)} fusion(f32[256,32,128]{2,0,1:T(8,128)S(1)} %get-tuple-element.16), kind=kOutput, calls=%fused_computation.47 | convolution fusion | flops 402667520 | bytes 8388608 | tf_op jit(solution)/shard_map/ka,ckb->cab/dot_general | solution.py:30
  352.7 9.1 %multiply_bitcast_fusion.1 = f32[256,32,128]{2,1,0:T(8,128)} fusion(f32[256,128,32]{1,2,0:T(8,128)S(1)} %fusion.19, f32[256,32,128]{2,0,1:T(8,128)S(1)} %get-tuple-element.15), kind=kOutput, calls=%fused_computation.34 | convolution fusion | flops 404764672 | bytes 12582912 | tf_op jit(solution)/shard_map/ka,ckb->cab/dot_general | solution.py:30
  361.8 5.0 mul.871
  366.7 10.4 %copy.216 = f32[1,256,4096]{1,0,2:T(1,128)} copy(f32[1,256,4096]{2,1,0:T(8,128)} %mul.871) | data formatting | bytes 8388608 | tf_op jit(solution)/shard_map/mul | solution.py:80
  377.2 11.8 %multiply_bitcast_fusion = f32[256,32,128]{2,1,0:T(8,128)} fusion(f32[256,128,32]{1,2,0:T(8,128)} %fusion.17, f32[256,32,128]{2,0,1:T(8,128)} %copy-done), kind=kOutput, calls=%fused_computation.33 | convolution fusion | flops 404764672 | bytes 12582912 | tf_op jit(solution)/shard_map/ka,ckb->cab/dot_general | solution.py:30
  388.9 4.9 mul.874
  393.9 10.1 %copy.217 = f32[1,256,4096]{1,0,2:T(1,128)} copy(f32[1,256,4096]{2,1,0:T(8,128)} %mul.874) | data formatting | bytes 8388608 | tf_op jit(solution)/shard_map/mul | solution.py:80
  404.0 9.9 %maximum_bitcast_fusion = f32[2,1,256,4096]{2,0,1,3:T(2,128)} fusion(f32[1,256,4096]{1,0,2:T(1,128)} %copy.217, f32[1,256,4096]{1,0,2:T(1,128)} %copy.216), kind=kLoop, calls=%fused_computation.3 | loop fusion | flops 2097152 | bytes 16777216 | tf_op jit(solution)/shard_map/broadcast_in_dim | solution.py:108
  413.9 6.1 all-to-all-start.2
  420.4 16.6 %fusion.396 = (f32[1024,1024]{1,0:T(8,128)}, f32[1024,1024]{1,0:T(8,128)}) fusion(f32[1024,1024]{1,0:T(8,128)} %param.7), kind=kLoop, calls=%fused_computation.412 | loop fusion | bytes 12582912 | tf_op jit(solution)/shard_map/sin | solution.py:112
  437.0 76.2 %all-to-all-done.2 = f32[2,1,256,4096]{2,0,1,3:T(2,128)} async-done(((f32[2,1,256,4096]{2,0,1,3:T(2,128)}), f32[2,1,256,4096]{2,0,1,3:T(2,128)}, u32[]{:S(2)}, u32[]{:S(2)}) %all-to-all-start.2) | async-done | bytes 8388640 | tf_op jit(solution)/shard_map/all_to_all | solution.py:107
  513.2 11.7 %fusion.394 = (f32[1,4,1,256,1024]{3,0,4,1,2:T(1,128)}, f32[1,4,1,256,1024]{3,0,4,1,2:T(1,128)}) fusion(f32[2,4,1,256,1024]{3,0,4,1,2:T(2,128)} %bitcast.38), kind=kLoop, calls=%fused_computation.410 | loop fusion | bytes 16777216 | tf_op jit(solution)/shard_map/slice | solution.py:112
  524.8 10.9 %copy.218 = f32[1,4,1,256,1024]{4,3,1,2,0:T(8,128)} copy(f32[1,4,1,256,1024]{3,0,4,1,2:T(1,128)} %get-tuple-element.19) | data formatting | bytes 8388608 | tf_op jit(solution)/shard_map/slice | solution.py:112
  535.8 11.0 %copy.219 = f32[1,4,1,256,1024]{4,3,1,2,0:T(8,128)} copy(f32[1,4,1,256,1024]{3,0,4,1,2:T(1,128)} %get-tuple-element.20) | data formatting | bytes 8388608 | tf_op jit(solution)/shard_map/slice | solution.py:112
  546.7 10.4 %fusion.1 = (f32[1024,1024]{1,0:T(8,128)S(1)}, f32[1024,1024]{1,0:T(8,128)}) fusion(f32[1024,1024]{1,0:T(8,128)} %get-tuple-element.23, f32[1,4,1,256,1024]{4,3,1,2,0:T(8,128)} %copy.219, f32[1024,1024]{1,0:T(8,128)} %get-tuple-element.24, f32[1,4,1,256,1024]{4,3,1,2,0:T(8,128)} %copy.218), kind=kLoop, calls=%fused_computation.9 | loop fusion | flops 6291456 | bytes 25165824 | tf_op jit(solution)/shard_map/sub | solution.py:40
  557.1 8.4 %fusion.11 = f32[8,128,1024]{2,0,1:T(8,128)S(1)} fusion(f32[8,128,1024]{2,1,0:T(8,128)} %bitcast.210), kind=kOutput, calls=%fused_computation.41 | convolution fusion | flops 100664192 | bytes 8388608 | tf_op jit(solution)/shard_map/ka,abc->kbc/dot_general | solution.py:30
  565.6 6.3 fusion.9
  571.9 6.5 fusion.83
  578.4 7.2 %multiply_subtract_fusion = (f32[8,128,1024]{2,0,1:T(8,128)S(1)}, f32[8,128,1024]{2,0,1:T(8,128)S(1)}) fusion(f32[8,128,1024]{2,0,1:T(8,128)S(1)} %fusion.83, f32[8,128]{0,1:T(8,128)S(1)} %copy.225, f32[8,128]{0,1:T(8,128)S(1)} %copy.222, f32[8,128,1024]{2,0,1:T(8,128)S(1)} %fusion.9, f32[8,128,1024]{2,1,0:T(8,128)S(1)} %bitcast.207), kind=kOutput, calls=%fused_computation.32 | convolution fusion | flops 108004224 | bytes 20979712 | tf_op jit(solution)/shard_map/ka,abc->kbc/dot_general | solution.py:30
  585.7 4.9 fusion.51
  590.6 5.3 fusion.49
  595.9 5.0 fusion.99
  602.1 5.1 fusion.102
  609.0 4.5 collective-permute-start
  613.4 4.8 fusion.55
  618.2 4.9 fusion.93
  624.3 5.0 fusion.53
  629.3 4.9 fusion.96
  635.4 67.2 %collective-permute-done = f32[2,512,1024]{2,1,0:T(8,128)S(1)} collective-permute-done((f32[2,512,1024]{2,1,0:T(8,128)S(1)}, f32[2,512,1024]{2,1,0:T(8,128)S(1)}, u32[]{:S(2)}, u32[]{:S(2)}) %collective-permute-start) | collective-permute-done | bytes 4194336 | tf_op jit(solution)/shard_map/ppermute | solution.py:12
  (43 shorter events, 31.7 us)
Async XLA Ops:
  7.2 53.8 %all-to-all-start = ((f32[2,128,4096]{1,0,2:T(2,128)}), f32[2,128,4096]{1,0,2:T(2,128)}, u32[]{:S(2)}, u32[]{:S(2)}) async-start(f32[2,128,4096]{1,0,2:T(2,128)} %copy.181), calls=%async_computation | async-start | bytes 8388608 | tf_op jit(solution)/shard_map/all_to_all | solution.py:85
  119.7 6.6 copy-start.7
  119.7 6.6 copy-start.8
  140.1 98.8 %all-to-all-start.1 = ((f32[2,4,256,1024]{3,2,0,1:T(8,128)}), f32[2,4,256,1024]{3,2,0,1:T(8,128)}, u32[]{:S(2)}, u32[]{:S(2)}) async-start(f32[2,4,256,1024]{3,2,0,1:T(8,128)} %pad_maximum_fusion), calls=%async_computation.1 | async-start | bytes 16777216 | tf_op jit(solution)/shard_map/all_to_all | solution.py:95
  256.0 8.1 %copy-start.9 = (f32[1,1,256,4,1024]{4,2,0,3,1:T(8,128)S(1)}, f32[1,1,256,4,1024]{4,2,0,3,1:T(8,128)}, u32[]{:S(2)}) copy-start(f32[1,1,256,4,1024]{4,2,0,3,1:T(8,128)} %get-tuple-element.22) | copy-start | bytes 12582916
  274.3 6.3 copy-start.2
  274.3 6.3 copy-start.6
  280.6 4.0 copy-start.1
  304.9 6.9 copy-start.4
  305.0 6.9 copy-start.5
  337.2 15.5 %copy-start = (f32[256,32,128]{2,0,1:T(8,128)}, f32[256,32,128]{2,0,1:T(8,128)S(1)}, u32[]{:S(2)}) copy-start(f32[256,32,128]{2,0,1:T(8,128)S(1)} %get-tuple-element.15) | copy-start | bytes 12582916
  413.9 99.2 %all-to-all-start.2 = ((f32[2,1,256,4096]{2,0,1,3:T(2,128)}), f32[2,1,256,4096]{2,0,1,3:T(2,128)}, u32[]{:S(2)}, u32[]{:S(2)}) async-start(f32[2,1,256,4096]{2,0,1,3:T(2,128)} %maximum_bitcast_fusion), calls=%async_computation.2 | async-start | bytes 16777216 | tf_op jit(solution)/shard_map/all_to_all | solution.py:107
  557.1 8.4 %copy-start.3 = (f32[1024,1024]{1,0:T(8,128)S(1)}, f32[1024,1024]{1,0:T(8,128)}, u32[]{:S(2)}) copy-start(f32[1024,1024]{1,0:T(8,128)} %get-tuple-element.6) | copy-start | bytes 12582916
  609.0 93.7 %collective-permute-start = (f32[2,512,1024]{2,1,0:T(8,128)S(1)}, f32[2,512,1024]{2,1,0:T(8,128)S(1)}, u32[]{:S(2)}, u32[]{:S(2)}) collective-permute-start(f32[2,512,1024]{2,1,0:T(8,128)S(1)} %maximum_multiply_fusion.1), channel_id=1, source_target_pairs={{0,4},{4,8},{8,12},{1,5},{5,9},{9,13},{2,6},{6,10},{10,14},{3,7},{... | collective-permute-start | bytes 12582920 | tf_op jit(solution)/shard_map/ppermute | solution.py:12
where the time goes:
time: 718 us; the launch traced here: 706 us
  waiting for transfers between devices  236 us (33%)
  matrix products  227 us (32%)
  local copies, waits for them, and re-layouts  183 us (25%)
  other arithmetic  38.1 us (5%)
  starting transfers between devices  21.1 us (3%)
    dot_general x36, matrix products, mixing(): return jnp.einsum(spec, left, right, precision=lax.Precision.HIGHEST)  227 us
    all_to_all x1, waiting for transfers between devices, body(): lax.all_to_all(jnp.stack(filtered)[:, None], 'tile', split_axis=3, concat...  76.2 us
    ppermute x1, waiting for transfers between devices, from_behind(): return lax.ppermute(value, axis, pairs)  67.2 us
    all_to_all x1, waiting for transfers between devices, body(): lax.all_to_all(grouped, 'tile', split_axis=1, concat_axis=3, tiled=True)  60.2 us
    all_to_all x1, waiting for transfers between devices, body(): lax.all_to_all(raw_echo, 'tile', split_axis=2, concat_axis=1, tiled=True)  32 us
    slice x2, local copies, waits for them, and re-layouts, body(): returned[0]  22.6 us
    cos x2, local copies, waits for them, and re-layouts, body(): spectral = rotate(spectral, (jnp.cos(permuted), jnp.sin(permuted)))  21.9 us
    sub x2, other arithmetic, rotate(): values[0] * table[0] - values[1] * table[1]  20 us
  transfers between devices with their start and end apart: 4, of which 4 were waited for; matrix products, arithmetic and copies ran while one was open for 13% of the time, Pallas kernels for 0%

commit v1 on v0

v1 whole, which is shorter than its diff:
```python
import functools
import math

import jax
import jax.numpy as jnp
import numpy as np
from jax import lax
from jax.experimental import pallas as pl
from jax.experimental.pallas import tpu as pltpu
from jax.sharding import PartitionSpec as P

F32 = jnp.float32
BF16 = jnp.bfloat16
LANES = 128


def halves(table):
    hi = np.asarray(table, np.float32).astype(jnp.bfloat16)
    lo = (np.asarray(table, np.float64) - hi.astype(np.float64)).astype(jnp.bfloat16)
    return np.stack([hi, lo])


def roots(rows, cols, modulus, direction):
    residue = np.outer(rows, cols) % modulus
    angle = residue * (direction * 2.0 * math.pi / modulus)
    return np.cos(angle), np.sin(angle)


def left_table(rows, cols, modulus, direction, scale=1.0):
    c, s = roots(rows, cols, modulus, direction)
    return halves(np.block([[c, -s], [s, c]]) * scale)


def right_table(rows, cols, modulus, direction, scale=1.0):
    c, s = roots(rows, cols, modulus, direction)
    return halves(np.block([[c, s], [-s, c]]) * scale)


def twist_table(count, length, modulus, direction):
    c, s = roots(np.arange(count), np.arange(length), modulus, direction)
    full = np.stack([c, s]).astype(np.float32)
    return np.ascontiguousarray(np.broadcast_to(full[..., None], full.shape + (LANES,)))


def split(x):
    hi = x.astype(BF16)
    return hi, (x - hi.astype(F32)).astype(BF16)


def mm(a, b):
    return jnp.dot(a, b, preferred_element_type=F32)


def times(a, t):
    return a[0] * t[0] - a[1] * t[1], a[0] * t[1] + a[1] * t[0]


def plus(a, b):
    return a[0] + b[0], a[1] + b[1]


def minus(a, b):
    return a[0] - b[0], a[1] - b[1]


def quarter(a, direction):
    return (-a[1], a[0]) if direction > 0 else (a[1], -a[0])


def four(v, direction):
    a, b = plus(v[0], v[2]), minus(v[0], v[2])
    c, d = plus(v[1], v[3]), quarter(minus(v[1], v[3]), direction)
    return [plus(a, c), plus(b, d), minus(a, c), minus(b, d)]


def fft(v, direction):
    n = len(v)
    if n == 1:
        return v
    if n == 2:
        return [plus(v[0], v[1]), minus(v[0], v[1])]
    if n == 4:
        return four(v, direction)
    parts = [fft(v[e::4], direction) for e in range(4)] if n % 4 == 0 else None
    out = [None] * n
    m = n // 4
    for f in range(m):
        items = []
        for e in range(4):
            x = parts[e][f]
            k = e * f % n
            if k == 0:
                pass
            elif 8 * k == n:
                h = np.float32(math.sqrt(0.5))
                q = quarter(x, direction)
                x = ((x[0] + q[0]) * h, (x[1] + q[1]) * h)
            elif 4 * k == n:
                x = quarter(x, direction)
            elif 8 * k == 3 * n:
                h = np.float32(math.sqrt(0.5))
                q = quarter(x, direction)
                x = ((q[0] - x[0]) * h, (q[1] - x[1]) * h)
            else:
                ang = direction * 2.0 * math.pi * k / n
                x = times(x, (np.float32(math.cos(ang)), np.float32(math.sin(ang))))
            items.append(x)
        got = four(items, direction)
        for j in range(4):
            out[f + j * m] = got[j]
    return out


def front_kernel(x_ref, table_ref, twist_ref, cos_ref, sin_ref, o_ref):
    q = x_ref.shape[1] // 4
    m = o_ref.shape[1] // 4
    width = x_ref.shape[2]
    hi, lo = table_ref[0], table_ref[1]
    z = []
    for e in range(4):
        rows = pl.ds(e, q, stride=4)
        s = jnp.concatenate([x_ref[0, rows, :], x_ref[1, rows, :]], axis=0)
        s_hi, s_lo = split(s)
        r = mm(hi, s_hi) + mm(hi, s_lo) + mm(lo, s_hi)
        r = (r[:m], r[m:])
        if e:
            r = times(r, (twist_ref[0, e], twist_ref[1, e]))
        z.append(r)
    for j, x in enumerate(four(z, -1)):
        rows = pl.ds(j * m, m)
        x = times(x, (cos_ref[rows, :], sin_ref[rows, :]))
        o_ref[0, rows, :] = x[0]
        o_ref[1, rows, :] = x[1]


def back_kernel(x_ref, table_ref, twist_ref, cos_ref, sin_ref, o_ref):
    m = x_ref.shape[1] // 4
    q = o_ref.shape[1] // 4
    hi, lo = table_ref[0], table_ref[1]
    v = []
    for j in range(4):
        rows = pl.ds(j * m, m)
        v.append(times((x_ref[0, rows, :], x_ref[1, rows, :]), (cos_ref[rows, :], sin_ref[rows, :])))
    for e, x in enumerate(four(v, 1)):
        if e:
            x = times(x, (twist_ref[0, e], twist_ref[1, e]))
        s_hi, s_lo = split(jnp.concatenate(x, axis=0))
        r = mm(hi, s_hi) + mm(hi, s_lo) + mm(lo, s_hi)
        rows = pl.ds(e, q, stride=4)
        o_ref[0, rows, :] = r[:q]
        o_ref[1, rows, :] = r[q:]


def range_kernel(x_ref, fwd_ref, inv_ref, twist_ref, cos_ref, sin_ref, o_ref, hi_ref, lo_ref, mid_ref):
    block = x_ref.shape[1]
    n_one = cos_ref.shape[0]
    step = 16
    f_hi, f_lo = fwd_ref[0], fwd_ref[1]
    b_hi, b_lo = inv_ref[0], inv_ref[1]

    @pl.loop(0, block // step)
    def _(i):
        rows = pl.ds(pl.multiple_of(i * step, step), step)
        v = [
            tuple(x_ref[c, rows, pl.ds(a * LANES, LANES)] for c in (0, 1))
            for a in range(n_one)
        ]
        for k, x in enumerate(fft(v, -1)):
            if k:
                x = times(x, (twist_ref[0, k : k + 1, :], twist_ref[1, k : k + 1, :]))
            for c in (0, 1):
                h, l = split(x[c])
                hi_ref[k, rows, pl.ds(c * LANES, LANES)] = h
                lo_ref[k, rows, pl.ds(c * LANES, LANES)] = l

    group = 4

    @pl.loop(0, n_one // group)
    def _(i):
        ks = pl.ds(i * group, group)
        flat = (group * block, 2 * LANES)
        h, l = hi_ref[ks].reshape(flat), lo_ref[ks].reshape(flat)
        r = mm(h, f_hi) + mm(l, f_hi) + mm(h, f_lo)
        c = cos_ref[ks].reshape(group * block, LANES)
        s = sin_ref[ks].reshape(group * block, LANES)
        r = times((r[:, :LANES], r[:, LANES:]), (c, s))
        h, l = split(jnp.concatenate(r, axis=1))
        r = mm(h, b_hi) + mm(l, b_hi) + mm(h, b_lo)
        mid_ref[ks] = r.reshape(group, block, 2 * LANES)

    @pl.loop(0, block // 8)
    def _(i):
        rows = pl.ds(pl.multiple_of(i * 8, 8), 8)
        v = []
        for k in range(n_one):
            x = tuple(mid_ref[k, rows, pl.ds(c * LANES, LANES)] for c in (0, 1))
            if k:
                x = times(x, (twist_ref[0, k : k + 1, :], -twist_ref[1, k : k + 1, :]))
            v.append(x)
        for a, x in enumerate(fft(v, 1)):
            for c in (0, 1):
                o_ref[c, rows, pl.ds(a * LANES, LANES)] = x[c]


def azimuth(kernel, x, table, twist, cos, sin, rows):
    width = x.shape[2]
    tile = LANES
    whole = lambda a: pl.BlockSpec(a.shape, lambda i: (0,) * a.ndim)
    return pl.pallas_call(
        kernel,
        grid=(width // tile,),
        out_shape=jax.ShapeDtypeStruct((2, rows, width), F32),
        in_specs=[
            pl.BlockSpec((2, x.shape[1], tile), lambda i: (0, 0, i)),
            whole(table),
            whole(twist),
            pl.BlockSpec((cos.shape[0], tile), lambda i: (0, i)),
            pl.BlockSpec((cos.shape[0], tile), lambda i: (0, i)),
        ],
        out_specs=pl.BlockSpec((2, rows, tile), lambda i: (0, 0, i)),
        compiler_params=pltpu.CompilerParams(vmem_limit_bytes=48 << 20),
        cost_estimate=pl.CostEstimate(
            flops=6 * table.shape[1] * table.shape[2] * 4 * width,
            bytes_accessed=4 * (x.size + 2 * cos.size + 2 * rows * width),
            transcendentals=0,
        ),
    )(x, table, twist, cos, sin)


def range_filter(x, fwd, inv, twist, cos, sin):
    _, count, extent = x.shape
    n_one = extent // LANES
    block = min(64, count)
    whole = lambda a: pl.BlockSpec(a.shape, lambda i: (0,) * a.ndim)
    return pl.pallas_call(
        range_kernel,
        grid=(count // block,),
        out_shape=jax.ShapeDtypeStruct(x.shape, F32),
        in_specs=[
            pl.BlockSpec((2, block, extent), lambda i: (0, i, 0)),
            whole(fwd),
            whole(inv),
            whole(twist),
            pl.BlockSpec((n_one, block, LANES), lambda i: (0, i, 0)),
            pl.BlockSpec((n_one, block, LANES), lambda i: (0, i, 0)),
        ],
        out_specs=pl.BlockSpec((2, block, extent), lambda i: (0, i, 0)),
        scratch_shapes=[
            pltpu.VMEM((n_one, block, 2 * LANES), BF16),
            pltpu.VMEM((n_one, block, 2 * LANES), BF16),
            pltpu.VMEM((n_one, block, 2 * LANES), F32),
        ],
        compiler_params=pltpu.CompilerParams(vmem_limit_bytes=48 << 20),
        cost_estimate=pl.CostEstimate(
            flops=12 * x.size * 256, bytes_accessed=4 * 3 * x.size, transcendentals=0
        ),
    )(x, fwd, inv, twist, cos, sin)


def body(raw_echo, phase_scaling, phase_range, phase_azimuth):
    tiles = lax.axis_size("tile")
    columns = lax.all_to_all(raw_echo, "tile", split_axis=2, concat_axis=1, tiled=True)
    pulses, width = columns.shape[1:]
    extent = phase_scaling.shape[0]
    m, q = extent // 4, pulses // 4
    count, ranges = phase_range.shape
    n_one = ranges // LANES
    rows = np.arange(m)
    table = left_table(rows, np.arange(q), m, -1)
    spectrum = azimuth(
        front_kernel, columns, table, twist_table(4, m, extent, -1),
        jnp.cos(phase_scaling), jnp.sin(phase_scaling), extent,
    )
    grouped = spectrum.reshape(2, tiles, extent // tiles, width)
    doppler = lax.all_to_all(grouped, "tile", split_axis=1, concat_axis=3, tiled=True)
    permuted = phase_range.reshape(count, LANES, n_one).transpose(2, 0, 1)
    lane = np.arange(LANES)
    c, s = roots(np.arange(n_one), lane, ranges, -1)
    filtered = range_filter(
        doppler.reshape(2, count, ranges),
        right_table(lane, lane, LANES, -1),
        right_table(lane, lane, LANES, 1, 1.0 / ranges),
        np.stack([c, s]).astype(np.float32),
        jnp.cos(permuted), jnp.sin(permuted),
    )
    returned = lax.all_to_all(filtered[:, None], "tile", split_axis=3, concat_axis=1, tiled=True)
    returned = returned.reshape(2, extent, width)
    twist = twist_table(4, m, extent, 1)
    cos, sin = jnp.cos(phase_azimuth), jnp.sin(phase_azimuth)
    rest = azimuth(
        back_kernel, returned, left_table(rows[q:], rows, m, 1, 1.0 / extent), twist,
        cos, sin, extent - pulses,
    )
    length = lax.axis_size("az")
    incoming = lax.ppermute(rest, "az", [(i, i + 1) for i in range(length - 1)])
    head = azimuth(
        back_kernel, returned, left_table(rows[:q], rows, m, 1, 1.0 / extent), twist,
        cos, sin, pulses,
    )
    tail = extent - pulses
    if tail == pulses:
        return head + incoming
    return jnp.concatenate([head[:, :tail] + incoming, head[:, tail:]], axis=1)


def solution(mesh):
    return jax.shard_map(
        body,
        mesh=mesh,
        in_specs=(
            P(None, ("strip", "az", "tile"), None),
            P(None, "tile"),
            P("tile", None),
            P(None, "tile"),
        ),
        out_specs=P(None, ("strip", "az"), "tile"),
        check_vma=False,
    )
```

time: 718 us -> 485 us (0.68); the launches traced: 706 us -> 483 us
  matrix products: 227 us -> 0 us
  Pallas kernels: 0 us -> 69.9 us
  local copies, waits for them, and re-layouts: 183 us -> 143 us
  other arithmetic: 38.1 us -> 3.38 us
  waiting for transfers between devices: 236 us -> 245 us
    dot_general x36 -> x0, matrix products: 227 us -> none  [mixing(): return jnp.einsum(spec, left, right, precision=lax.Precision.HIGHEST)]
    pallas_call x0 -> x4, Pallas kernels: none -> 69.9 us  [the longest x3 38.2 us: azimuth(): pl.pallas_call(kernel, grid=(width // tile,), out_shape=jax.ShapeDtypeStr...]
    slice x7 -> x0, local copies, waits for them, and re-layouts: 53 us -> none  [the longest x2 22.6 us: body(): returned[0]]
    mul x4 -> x0, local copies, waits for them, and re-layouts: 30.5 us -> none  [the longest x2 15.4 us: range_inverse(): mixed[0].reshape(width, extent) * scale]
    all_to_all x0 -> x2, local copies, waits for them, and re-layouts: none -> 25.3 us  [the longest x1 13.3 us: body(): lax.all_to_all(filtered[:, None], 'tile', split_axis=3, concat_axis=1, ti...]
    sub x2 -> x0, other arithmetic: 20 us -> none  [rotate(): values[0] * table[0] - values[1] * table[1]]
    reshape x0 -> x2, local copies, waits for them, and re-layouts: none -> 19.2 us  [the longest x1 10.9 us: body(): doppler.reshape(2, count, ranges)]
    cos x4 -> x1, local copies, waits for them, and re-layouts: 22.1 us -> 5.32 us  [body(): jnp.cos(permuted)]
  transfers between devices with their start and end apart: 4 -> 4, of which waited for: 4 -> 4; matrix products, arithmetic and copies ran while one was open for 13% -> 14% of each run, Pallas kernels for 0% -> 3%
where the time goes in v1:
time: 485 us; the launch traced here: 483 us
  waiting for transfers between devices  245 us (51%)
  local copies, waits for them, and re-layouts  143 us (29%)
  Pallas kernels  69.9 us (14%)
  starting transfers between devices  21.1 us (4%)
    ppermute x1, waiting for transfers between devices, body(): incoming = lax.ppermute(rest, 'az', [(i, i + 1) for i in range(length - 1)])  76.7 us
    all_to_all x1, waiting for transfers between devices, body(): lax.all_to_all(filtered[:, None], 'tile', split_axis=3, concat_axis=1, ti...  76.3 us
    all_to_all x1, waiting for transfers between devices, body(): lax.all_to_all(grouped, 'tile', split_axis=1, concat_axis=3, tiled=True)  60 us
    pallas_call x3, Pallas kernels, azimuth(): pl.pallas_call(kernel, grid=(width // tile,), out_shape=jax.ShapeDtypeStr...  38.2 us
    all_to_all x1, waiting for transfers between devices, body(): lax.all_to_all(raw_echo, 'tile', split_axis=2, concat_axis=1, tiled=True)  32.3 us
    pallas_call x1, Pallas kernels, range_filter(): pl.pallas_call(range_kernel, grid=(count // block,), out_shape=jax.ShapeD...  31.7 us
    sin x2, local copies, waits for them, and re-layouts, body(): jnp.sin(permuted)  22 us
    unnamed x22, local copies, waits for them, and re-layouts  17.2 us
  transfers between devices with their start and end apart: 4, of which 4 were waited for; matrix products, arithmetic and copies ran while one was open for 14% of the time, Pallas kernels for 3%

profile of v1, /device:TPU:0, one launch (start us, length us, event | category | flops | bytes accessed | tf_op | source)
XLA Modules:
  0.0 482.6 jit_solution(6469092128483657745)
XLA Ops:
  0.0 7.2 %copy.23 = f32[2,128,4096]{1,0,2:T(2,128)} copy(f32[2,128,4096]{2,1,0:T(8,128)} %param.12) | data formatting | bytes 8388608 | tf_op args[0]
  7.2 4.8 %all-to-all-start = ((f32[2,128,4096]{1,0,2:T(2,128)}), f32[2,128,4096]{1,0,2:T(2,128)}, u32[]{:S(2)}, u32[]{:S(2)}) async-start(f32[2,128,4096]{1,0,2:T(2,128)} %copy.23), calls=%async_computation | async-start | bytes 8388608 | tf_op jit(solution)/shard_map/all_to_all | solution.py:262
  12.0 16.6 %fusion.2 = (f32[1024,1024]{1,0:T(8,128)}, f32[1024,1024]{1,0:T(8,128)}) fusion(f32[1024,1024]{1,0:T(8,128)} %param.13), kind=kLoop, calls=%fused_computation.2 | loop fusion | bytes 12582912 | tf_op jit(solution)/shard_map/sin | solution.py:272
  28.7 32.3 %all-to-all-done = f32[2,128,4096]{1,0,2:T(2,128)} async-done(((f32[2,128,4096]{1,0,2:T(2,128)}), f32[2,128,4096]{1,0,2:T(2,128)}, u32[]{:S(2)}, u32[]{:S(2)}) %all-to-all-start) | async-done | bytes 4194336 | tf_op jit(solution)/shard_map/all_to_all | solution.py:262
  60.9 0.0 copy-start.3
  60.9 0.0 copy-start.6
  60.9 7.3 %copy.24 = f32[2,128,4,1024]{3,1,2,0:T(8,128)} copy(f32[2,128,4,1024]{1,0,3,2:T(2,128)} %bitcast) | data formatting | bytes 8388608 | tf_op jit(solution)/shard_map/all_to_all | solution.py:262
  68.3 0.0 copy-done.3
  68.3 0.0 copy-done.6
  68.3 0.0 copy-start.1
  68.3 2.2 copy-done.1
  70.5 13.1 %shard_map.118 = f32[2,1024,1024]{2,1,0:T(8,128)} custom-call(f32[2,512,1024]{2,1,0:T(8,128)S(1)} %bitcast.20, bf16[2,512,256]{2,1,0:T(8,128)(2,1)S(1)} %copy-done.6, f32[2,4,256,128]{3,2,1,0:T(8,128)S(1)} %copy-done.3, f32[1024,1024]{1,0:T(8,128)} %get-tuple-element.10.cos_ref, f32[1024,1024]{1,0:T(8,128)} %get-tuple-element.9.sin_ref), custom_call_target="tpu_custom_call" | custom-call | flops 3221225472 | bytes 20971520 | tf_op jit(solution)/shard_map/pallas_call | solution.py:209
  83.6 8.3 %copy.25 = f32[2,4,256,1024]{3,2,0,1:T(8,128)} copy(f32[2,4,256,1024]{3,2,1,0:T(8,128)} %bitcast.24) | data formatting | bytes 16777216 | tf_op jit(solution)/shard_map/reshape | solution.py:274
  91.9 5.9 %all-to-all-start.1 = ((f32[2,4,256,1024]{3,2,0,1:T(8,128)}), f32[2,4,256,1024]{3,2,0,1:T(8,128)}, u32[]{:S(2)}, u32[]{:S(2)}) async-start(f32[2,4,256,1024]{3,2,0,1:T(8,128)} %copy.25), calls=%async_computation.1 | async-start | bytes 16777216 | tf_op jit(solution)/shard_map/all_to_all | solution.py:275
  97.7 5.6 %copy.27 = f32[256,4096]{0,1:T(8,128)} copy(f32[256,4096]{1,0:T(8,128)} %param.14) | data formatting | bytes 8388608 | tf_op args[2]
  103.4 16.6 %fusion.1 = (f32[256,4096]{0,1:T(8,128)}, f32[256,4096]{0,1:T(8,128)}) fusion(f32[256,4096]{0,1:T(8,128)} %copy.27), kind=kLoop, calls=%fused_computation.1 | loop fusion | bytes 12582912 | tf_op jit(solution)/shard_map/sin | solution.py:284
  120.0 5.3 %copy.28 = f32[256,128,32]{1,0,2:T(8,128)} copy(f32[256,128,32]{0,2,1:T(8,128)} %bitcast.27) | data formatting | bytes 8388608 | tf_op jit(solution)/shard_map/cos | solution.py:284
  125.3 5.4 %copy.30 = f32[256,128,32]{1,0,2:T(8,128)} copy(f32[256,128,32]{0,2,1:T(8,128)} %bitcast.26) | data formatting | bytes 8388608 | tf_op jit(solution)/shard_map/sin | solution.py:284
  130.7 60.0 %all-to-all-done.1 = f32[2,4,256,1024]{3,2,0,1:T(8,128)} async-done(((f32[2,4,256,1024]{3,2,0,1:T(8,128)}), f32[2,4,256,1024]{3,2,0,1:T(8,128)}, u32[]{:S(2)}, u32[]{:S(2)}) %all-to-all-start.1) | async-done | bytes 8388640 | tf_op jit(solution)/shard_map/all_to_all | solution.py:275
  190.7 12.0 %copy.26 = f32[2,1,256,4,1024]{4,3,2,0,1:T(4,128)} copy(f32[2,1,256,4,1024]{4,2,0,3,1:T(8,128)} %bitcast.5) | data formatting | bytes 16777216 | tf_op jit(solution)/shard_map/all_to_all | solution.py:275
  202.7 0.0 copy-start.7
  202.7 0.0 copy-start.8
  202.7 0.0 copy-start.9
  202.7 10.9 %reshape.15.x_ref = f32[2,256,4096]{2,1,0:T(8,128)} reshape(f32[2,1,256,4,1024]{4,3,2,0,1:T(4,128)} %copy.26) | data formatting | bytes 16777216 | tf_op jit(solution)/shard_map/reshape | solution.py:280
  213.6 0.0 copy-done.7
  213.6 0.0 copy-done.8
  213.6 0.0 copy-done.9
  213.7 0.0 copy-start
  213.7 2.2 copy-done
  215.8 31.7 %shard_map.119 = f32[2,256,4096]{2,1,0:T(8,128)} custom-call(f32[2,256,4096]{2,1,0:T(8,128)} %reshape.15.x_ref, bf16[2,256,256]{2,1,0:T(8,128)(2,1)S(1)} %copy-done.7, bf16[2,256,256]{2,1,0:T(8,128)(2,1)S(1)} %copy-done.8, f32[2,32,128]{2,1,0:T(8,128)S(1)} %copy-done.9, f32[32,256,128]{2,1,0:T(8,128)S(1)} %bitcast.19, f32[32,256,128]{2,1,0:T(8,128)} %bitcast.25), custom_call_target="tpu_custom_call" | custom-call | flops 6442450944 | bytes 25165824 | tf_op jit(solution)/shard_map/pallas_call | solution.py:235
  247.6 13.2 %copy.31 = f32[2,1,256,4096]{2,0,1,3:T(2,128)} copy(f32[2,1,256,4096]{3,2,0,1:T(8,128)} %bitcast.23) | data formatting | bytes 16777216 | tf_op jit(solution)/shard_map/broadcast_in_dim | solution.py:286
  260.7 5.9 %all-to-all-start.2 = ((f32[2,1,256,4096]{2,0,1,3:T(2,128)}), f32[2,1,256,4096]{2,0,1,3:T(2,128)}, u32[]{:S(2)}, u32[]{:S(2)}) async-start(f32[2,1,256,4096]{2,0,1,3:T(2,128)} %copy.31), calls=%async_computation.2 | async-start | bytes 16777216 | tf_op jit(solution)/shard_map/all_to_all | solution.py:286
  266.6 16.6 %fusion = (f32[1024,1024]{1,0:T(8,128)}, f32[1024,1024]{1,0:T(8,128)}) fusion(f32[1024,1024]{1,0:T(8,128)} %param.15), kind=kLoop, calls=%fused_computation | loop fusion | bytes 12582912 | tf_op jit(solution)/shard_map/sin | solution.py:289
  283.2 76.3 %all-to-all-done.2 = f32[2,1,256,4096]{2,0,1,3:T(2,128)} async-done(((f32[2,1,256,4096]{2,0,1,3:T(2,128)}), f32[2,1,256,4096]{2,0,1,3:T(2,128)}, u32[]{:S(2)}, u32[]{:S(2)}) %all-to-all-start.2) | async-done | bytes 8388640 | tf_op jit(solution)/shard_map/all_to_all | solution.py:286
  359.5 0.0 copy-start.2
  359.5 0.0 copy-start.5
  359.5 13.3 %copy.32 = f32[2,1,256,4,1024]{4,2,3,0,1:T(8,128)} copy(f32[2,1,256,4,1024]{2,0,4,3,1:T(2,128)} %bitcast.11) | data formatting | bytes 16777216 | tf_op jit(solution)/shard_map/all_to_all | solution.py:286
  372.8 0.0 copy-done.2
  372.8 0.0 copy-done.5
  372.9 0.0 copy-start.4
  372.9 12.5 %shard_map.121 = f32[2,512,1024]{2,1,0:T(8,128)S(1)} custom-call(f32[2,1024,1024]{2,1,0:T(8,128)} %bitcast.21, bf16[2,256,512]{2,1,0:T(8,128)(2,1)S(1)} %copy-done.5, f32[2,4,256,128]{3,2,1,0:T(8,128)S(1)} %copy-done.2, f32[1024,1024]{1,0:T(8,128)} %get-tuple-element.6.cos_ref, f32[1024,1024]{1,0:T(8,128)} %get-tuple-element.5.sin_ref), custom_call_target="tpu_custom_call" | custom-call | flops 3221225472 | bytes 20971520 | tf_op jit(solution)/shard_map/pallas_call | solution.py:209
  385.4 4.5 collective-permute-start
  389.9 0.0 copy-done.4
  389.9 12.5 %shard_map.120 = f32[2,512,1024]{2,1,0:T(8,128)S(1)} custom-call(f32[2,1024,1024]{2,1,0:T(8,128)} %bitcast.22, bf16[2,256,512]{2,1,0:T(8,128)(2,1)S(1)} %copy-done.4, f32[2,4,256,128]{3,2,1,0:T(8,128)S(1)} %copy-done.2, f32[1024,1024]{1,0:T(8,128)} %get-tuple-element.6.cos_ref, f32[1024,1024]{1,0:T(8,128)} %get-tuple-element.5.sin_ref), custom_call_target="tpu_custom_call" | custom-call | flops 3221225472 | bytes 20971520 | tf_op jit(solution)/shard_map/pallas_call | solution.py:209
  402.4 76.7 %collective-permute-done = f32[2,512,1024]{2,1,0:T(8,128)S(1)} collective-permute-done((f32[2,512,1024]{2,1,0:T(8,128)S(1)}, f32[2,512,1024]{2,1,0:T(8,128)S(1)}, u32[]{:S(2)}, u32[]{:S(2)}) %collective-permute-start) | collective-permute-done | bytes 4194336 | tf_op jit(solution)/shard_map/ppermute | solution.py:295
  479.2 3.4 add.3
Async XLA Ops:
  7.2 53.8 %all-to-all-start = ((f32[2,128,4096]{1,0,2:T(2,128)}), f32[2,128,4096]{1,0,2:T(2,128)}, u32[]{:S(2)}, u32[]{:S(2)}) async-start(f32[2,128,4096]{1,0,2:T(2,128)} %copy.23), calls=%async_computation | async-start | bytes 8388608 | tf_op jit(solution)/shard_map/all_to_all | solution.py:262
  60.9 7.3 %copy-start.3 = (f32[2,4,256,128]{3,2,1,0:T(8,128)S(1)}, f32[2,4,256,128]{3,2,1,0:T(8,128)}, u32[]{:S(2)}) copy-start(f32[2,4,256,128]{3,2,1,0:T(8,128)} %constant.17.clone.twist_ref) | copy-start | bytes 3145732
  60.9 7.3 %copy-start.6 = (bf16[2,512,256]{2,1,0:T(8,128)(2,1)S(1)}, bf16[2,512,256]{2,1,0:T(8,128)(2,1)}, u32[]{:S(2)}) copy-start(bf16[2,512,256]{2,1,0:T(8,128)(2,1)} %constant.16.clone.table_ref) | copy-start | bytes 1572868
  68.3 2.2 copy-start.1
  91.9 98.8 %all-to-all-start.1 = ((f32[2,4,256,1024]{3,2,0,1:T(8,128)}), f32[2,4,256,1024]{3,2,0,1:T(8,128)}, u32[]{:S(2)}, u32[]{:S(2)}) async-start(f32[2,4,256,1024]{3,2,0,1:T(8,128)} %copy.25), calls=%async_computation.1 | async-start | bytes 16777216 | tf_op jit(solution)/shard_map/all_to_all | solution.py:275
  202.7 10.9 %copy-start.7 = (bf16[2,256,256]{2,1,0:T(8,128)(2,1)S(1)}, bf16[2,256,256]{2,1,0:T(8,128)(2,1)}, u32[]{:S(2)}) copy-start(bf16[2,256,256]{2,1,0:T(8,128)(2,1)} %constant.18.clone.fwd_ref) | copy-start | bytes 786436
  202.7 10.9 %copy-start.8 = (bf16[2,256,256]{2,1,0:T(8,128)(2,1)S(1)}, bf16[2,256,256]{2,1,0:T(8,128)(2,1)}, u32[]{:S(2)}) copy-start(bf16[2,256,256]{2,1,0:T(8,128)(2,1)} %constant.19.clone.inv_ref) | copy-start | bytes 786436
  202.7 10.9 %copy-start.9 = (f32[2,32,128]{2,1,0:T(8,128)S(1)}, f32[2,32,128]{2,1,0:T(8,128)}, u32[]{:S(2)}) copy-start(f32[2,32,128]{2,1,0:T(8,128)} %constant.20.clone.twist_ref) | copy-start | bytes 98308
  213.7 2.2 copy-start
  260.7 98.8 %all-to-all-start.2 = ((f32[2,1,256,4096]{2,0,1,3:T(2,128)}), f32[2,1,256,4096]{2,0,1,3:T(2,128)}, u32[]{:S(2)}, u32[]{:S(2)}) async-start(f32[2,1,256,4096]{2,0,1,3:T(2,128)} %copy.31), calls=%async_computation.2 | async-start | bytes 16777216 | tf_op jit(solution)/shard_map/all_to_all | solution.py:286
  359.5 13.3 %copy-start.2 = (f32[2,4,256,128]{3,2,1,0:T(8,128)S(1)}, f32[2,4,256,128]{3,2,1,0:T(8,128)}, u32[]{:S(2)}) copy-start(f32[2,4,256,128]{3,2,1,0:T(8,128)} %constant.22.clone.twist_ref) | copy-start | bytes 3145732
  359.5 13.3 %copy-start.5 = (bf16[2,256,512]{2,1,0:T(8,128)(2,1)S(1)}, bf16[2,256,512]{2,1,0:T(8,128)(2,1)}, u32[]{:S(2)}) copy-start(bf16[2,256,512]{2,1,0:T(8,128)(2,1)} %constant.21.clone.table_ref) | copy-start | bytes 1572868
  372.9 17.1 %copy-start.4 = (bf16[2,256,512]{2,1,0:T(8,128)(2,1)S(1)}, bf16[2,256,512]{2,1,0:T(8,128)(2,1)}, u32[]{:S(2)}) copy-start(bf16[2,256,512]{2,1,0:T(8,128)(2,1)} %constant.23.clone.table_ref) | copy-start | bytes 1572868
  385.4 93.8 %collective-permute-start = (f32[2,512,1024]{2,1,0:T(8,128)S(1)}, f32[2,512,1024]{2,1,0:T(8,128)S(1)}, u32[]{:S(2)}, u32[]{:S(2)}) collective-permute-start(f32[2,512,1024]{2,1,0:T(8,128)S(1)} %shard_map.121), channel_id=1, source_target_pairs={{0,4},{4,8},{8,12},{1,5},{5,9},{9,13},{2,6},{6,10},{10,14},{3,7},{... | collective-permute-start | bytes 12582920 | tf_op jit(solution)/shard_map/ppermute | solution.py:295

commit v2 on v1

v2 whole, which is shorter than its diff:
```python
import functools
import math

import jax
import jax.numpy as jnp
import numpy as np
from jax import lax
from jax.experimental import pallas as pl
from jax.experimental.pallas import tpu as pltpu
from jax.sharding import PartitionSpec as P

F32 = jnp.float32
BF16 = jnp.bfloat16
LANES = 128


def halves(table):
    hi = np.asarray(table, np.float32).astype(jnp.bfloat16)
    lo = (np.asarray(table, np.float64) - hi.astype(np.float64)).astype(jnp.bfloat16)
    return np.stack([hi, lo])


def roots(rows, cols, modulus, direction):
    residue = np.outer(rows, cols) % modulus
    angle = residue * (direction * 2.0 * math.pi / modulus)
    return np.cos(angle), np.sin(angle)


def left_table(rows, cols, modulus, direction, scale=1.0):
    c, s = roots(rows, cols, modulus, direction)
    return halves(np.block([[c, -s], [s, c]]) * scale)


def right_table(rows, cols, modulus, direction, scale=1.0):
    c, s = roots(rows, cols, modulus, direction)
    return halves(np.block([[c, s], [-s, c]]) * scale)


def twist_table(count, length, modulus, direction):
    c, s = roots(np.arange(count), np.arange(length), modulus, direction)
    full = np.stack([c, s]).astype(np.float32)
    return np.ascontiguousarray(np.broadcast_to(full[..., None], full.shape + (LANES,)))


def split(x):
    hi = x.astype(BF16)
    return hi, (x - hi.astype(F32)).astype(BF16)


def mm(a, b):
    return jnp.dot(a, b, preferred_element_type=F32)


def times(a, t):
    return a[0] * t[0] - a[1] * t[1], a[0] * t[1] + a[1] * t[0]


def plus(a, b):
    return a[0] + b[0], a[1] + b[1]


def minus(a, b):
    return a[0] - b[0], a[1] - b[1]


def quarter(a, direction):
    return (-a[1], a[0]) if direction > 0 else (a[1], -a[0])


def four(v, direction):
    a, b = plus(v[0], v[2]), minus(v[0], v[2])
    c, d = plus(v[1], v[3]), quarter(minus(v[1], v[3]), direction)
    return [plus(a, c), plus(b, d), minus(a, c), minus(b, d)]


def fft(v, direction):
    n = len(v)
    if n == 1:
        return v
    if n == 2:
        return [plus(v[0], v[1]), minus(v[0], v[1])]
    if n == 4:
        return four(v, direction)
    parts = [fft(v[e::4], direction) for e in range(4)] if n % 4 == 0 else None
    out = [None] * n
    m = n // 4
    for f in range(m):
        items = []
        for e in range(4):
            x = parts[e][f]
            k = e * f % n
            if k == 0:
                pass
            elif 8 * k == n:
                h = np.float32(math.sqrt(0.5))
                q = quarter(x, direction)
                x = ((x[0] + q[0]) * h, (x[1] + q[1]) * h)
            elif 4 * k == n:
                x = quarter(x, direction)
            elif 8 * k == 3 * n:
                h = np.float32(math.sqrt(0.5))
                q = quarter(x, direction)
                x = ((q[0] - x[0]) * h, (q[1] - x[1]) * h)
            else:
                ang = direction * 2.0 * math.pi * k / n
                x = times(x, (np.float32(math.cos(ang)), np.float32(math.sin(ang))))
            items.append(x)
        got = four(items, direction)
        for j in range(4):
            out[f + j * m] = got[j]
    return out


def sincos(x):
    y = x * 0.5
    z = y * y
    s, c = -1.0 / 39916800, 1.0 / 479001600
    for a, b in ((362880, -3628800), (-5040, 40320), (120, -720), (-6, 24), (1, -2)):
        s = s * z + np.float32(1.0 / a)
        c = c * z + np.float32(1.0 / b)
    s = s * y
    c = c * z + 1.0
    return 1.0 - 2.0 * s * s, 2.0 * s * c


def greet(partners):
    barrier = pltpu.get_barrier_semaphore()
    for device in partners:
        pl.semaphore_signal(barrier, inc=1, device_id=device, device_id_type=pl.DeviceIdType.MESH)
    return barrier


def lanes(j):
    return pl.ds(pl.multiple_of(j * LANES, LANES), LANES)


def front_kernel(tiles, raw_ref, table_ref, twist_ref, phase_ref, o_ref, cols, send, recv, local):
    me = lax.axis_index("tile")
    rows_own = raw_ref.shape[1]
    m = o_ref.shape[1] // 4
    width = o_ref.shape[2]
    count = width // LANES
    own = pl.ds(pl.multiple_of(me * rows_own, rows_own), rows_own)

    def out(j, k):
        to = lax.rem(me + k, tiles)
        return pltpu.make_async_remote_copy(
            src_ref=raw_ref.at[:, :, lanes(to * count + j)],
            dst_ref=cols.at[j, :, own, :],
            send_sem=send.at[j, k - 1],
            recv_sem=recv.at[j, k - 1],
            device_id={"tile": to},
            device_id_type=pl.DeviceIdType.MESH,
        )

    def keep(j):
        return pltpu.make_async_copy(
            raw_ref.at[:, :, lanes(me * count + j)], cols.at[j, :, own, :], local.at[j]
        )

    barrier = greet([{"tile": lax.rem(me + k, tiles)} for k in range(1, tiles)])
    pl.semaphore_wait(barrier, tiles - 1)

    @pl.loop(0, count)
    def _(j):
        for k in range(1, tiles):
            out(j, k).start()
        keep(j).start()

    @pl.loop(0, count)
    def _(j):
        for k in range(1, tiles):
            out(j, k).wait_recv()
        keep(j).wait()
        hi, lo = table_ref[0], table_ref[1]
        q = cols.shape[2] // 4
        z = []
        for e in range(4):
            rows = pl.ds(e, q, stride=4)
            s = jnp.concatenate([cols[j, 0, rows, :], cols[j, 1, rows, :]], axis=0)
            s_hi, s_lo = split(s)
            r = mm(hi, s_hi) + mm(hi, s_lo) + mm(lo, s_hi)
            r = (r[:m], r[m:])
            if e:
                r = times(r, (twist_ref[0, e], twist_ref[1, e]))
            z.append(r)
        for f, x in enumerate(four(z, -1)):
            rows = pl.ds(f * m, m)
            x = times(x, sincos(phase_ref[rows, lanes(j)]))
            o_ref[0, rows, lanes(j)] = x[0]
            o_ref[1, rows, lanes(j)] = x[1]

    @pl.loop(0, count)
    def _(j):
        for k in range(1, tiles):
            out(j, k).wait_send()


def filter_rows(x_ref, base, block, fwd_ref, inv_ref, twist_ref, phase_ref, hi_ref, lo_ref, mid_ref):
    n_one = phase_ref.shape[0]
    step = 16
    f_hi, f_lo = fwd_ref[0], fwd_ref[1]
    b_hi, b_lo = inv_ref[0], inv_ref[1]

    @pl.loop(0, block // step)
    def _(i):
        rows = pl.ds(pl.multiple_of(i * step, step), step)
        at = pl.ds(pl.multiple_of(base + i * step, step), step)
        v = [
            tuple(x_ref[c, at, pl.ds(a * LANES, LANES)] for c in (0, 1))
            for a in range(n_one)
        ]
        for k, x in enumerate(fft(v, -1)):
            if k:
                x = times(x, (twist_ref[0, k : k + 1, :], twist_ref[1, k : k + 1, :]))
            for c in (0, 1):
                h, l = split(x[c])
                hi_ref[k, rows, pl.ds(c * LANES, LANES)] = h
                lo_ref[k, rows, pl.ds(c * LANES, LANES)] = l

    group = 4

    @pl.loop(0, n_one // group)
    def _(i):
        ks = pl.ds(i * group, group)
        flat = (group * block, 2 * LANES)
        h, l = hi_ref[ks].reshape(flat), lo_ref[ks].reshape(flat)
        r = mm(h, f_hi) + mm(l, f_hi) + mm(h, f_lo)
        turn = phase_ref[ks, pl.ds(pl.multiple_of(base, block), block), :]
        r = times((r[:, :LANES], r[:, LANES:]), sincos(turn.reshape(group * block, LANES)))
        h, l = split(jnp.concatenate(r, axis=1))
        r = mm(h, b_hi) + mm(l, b_hi) + mm(h, b_lo)
        mid_ref[ks] = r.reshape(group, block, 2 * LANES)

    @pl.loop(0, block // 8)
    def _(i):
        rows = pl.ds(pl.multiple_of(i * 8, 8), 8)
        at = pl.ds(pl.multiple_of(base + i * 8, 8), 8)
        v = []
        for k in range(n_one):
            x = tuple(mid_ref[k, rows, pl.ds(c * LANES, LANES)] for c in (0, 1))
            if k:
                x = times(x, (twist_ref[0, k : k + 1, :], -twist_ref[1, k : k + 1, :]))
            v.append(x)
        for a, x in enumerate(fft(v, 1)):
            for c in (0, 1):
                x_ref[c, at, pl.ds(a * LANES, LANES)] = x[c]


def back_kernel(
    tiles, length, block,
    spec_ref, turn_ref, phase_ref, fwd_ref, inv_ref, range_twist_ref, table_ref, twist_ref,
    o_ref,
    dop, ret, tail_out, tail_in, head, hi_ref, lo_ref, mid_ref,
    send_a, recv_a, local_a, send_b, recv_b, local_b, send_c, recv_c,
):
    me = lax.axis_index("tile")
    az = lax.axis_index("az")
    count = dop.shape[1]
    width = o_ref.shape[2]
    pulses = o_ref.shape[1]
    tail = tail_out.shape[2]
    blocks = count // block
    spans = width // LANES
    mine = pl.ds(pl.multiple_of(me * width, LANES), width)
    own = pl.ds(pl.multiple_of(me * count, count), count)

    def out(i, k):
        to = lax.rem(me + k, tiles)
        return pltpu.make_async_remote_copy(
            src_ref=spec_ref.at[:, pl.ds(pl.multiple_of(to * count + i * block, block), block), :],
            dst_ref=dop.at[:, pl.ds(pl.multiple_of(i * block, block), block), mine],
            send_sem=send_a.at[i, k - 1],
            recv_sem=recv_a.at[i, k - 1],
            device_id={"tile": to},
            device_id_type=pl.DeviceIdType.MESH,
        )

    def back(j, k):
        to = lax.rem(me + k, tiles)
        return pltpu.make_async_remote_copy(
            src_ref=dop.at[:, :, lanes(to * spans + j)],
            dst_ref=ret.at[j, :, own, :],
            send_sem=send_b.at[j, k - 1],
            recv_sem=recv_b.at[j, k - 1],
            device_id={"tile": to},
            device_id_type=pl.DeviceIdType.MESH,
        )

    def keep(j):
        return pltpu.make_async_copy(
            dop.at[:, :, lanes(me * spans + j)], ret.at[j, :, own, :], local_b.at[j]
        )

    def onward(j):
        return pltpu.make_async_remote_copy(
            src_ref=tail_out.at[j],
            dst_ref=tail_in.at[j],
            send_sem=send_c.at[j],
            recv_sem=recv_c.at[j],
            device_id={"az": lax.rem(az + 1, length)},
            device_id_type=pl.DeviceIdType.MESH,
        )

    barrier = greet(
        [{"tile": lax.rem(me + k, tiles)} for k in range(1, tiles)]
        + [{"az": lax.rem(az + 1, length)}, {"az": lax.rem(az + length - 1, length)}]
    )
    pl.semaphore_wait(barrier, tiles + 1)

    @pl.loop(0, blocks)
    def _(i):
        for k in range(1, tiles):
            out(i, k).start()

    first = pltpu.make_async_copy(spec_ref.at[:, own, :], dop.at[:, :, mine], local_a)
    first.start()
    first.wait()

    @pl.loop(0, blocks)
    def _(i):
        for k in range(1, tiles):
            out(i, k).wait_recv()
        filter_rows(
            dop, i * block, block, fwd_ref, inv_ref, range_twist_ref, turn_ref,
            hi_ref, lo_ref, mid_ref,
        )

    @pl.loop(0, spans)
    def _(j):
        for k in range(1, tiles):
            back(j, k).start()
        keep(j).start()

    @pl.loop(0, spans)
    def _(j):
        for k in range(1, tiles):
            back(j, k).wait_recv()
        keep(j).wait()
        m = ret.shape[2] // 4
        q = pulses // 4
        hi, lo = table_ref[0], table_ref[1]
        v = []
        for f in range(4):
            rows = pl.ds(f * m, m)
            v.append(times((ret[j, 0, rows, :], ret[j, 1, rows, :]), sincos(phase_ref[rows, lanes(j)])))
        for e, x in enumerate(four(v, 1)):
            if e:
                x = times(x, (twist_ref[0, e], twist_ref[1, e]))
            s_hi, s_lo = split(jnp.concatenate(x, axis=0))
            r = mm(hi, s_hi) + mm(hi, s_lo) + mm(lo, s_hi)
            for c in (0, 1):
                head[c, pl.ds(e, q, stride=4), :] = r[c * m : c * m + q]
                tail_out[j, c, pl.ds(e, m - q, stride=4), :] = r[c * m + q : (c + 1) * m]

        @pl.when(az < length - 1)
        def _():
            onward(j).start()

        o_ref[:, :, lanes(j)] = head[...]

    @pl.when(az > 0)
    def _():
        @pl.loop(0, spans)
        def _(j):
            onward(j).wait_recv()
            o_ref[:, pl.ds(0, tail), lanes(j)] += tail_in[j]

    @pl.loop(0, blocks)
    def _(i):
        for k in range(1, tiles):
            out(i, k).wait_send()

    @pl.loop(0, spans)
    def _(j):
        for k in range(1, tiles):
            back(j, k).wait_send()

    @pl.when(az < length - 1)
    def _():
        @pl.loop(0, spans)
        def _(j):
            onward(j).wait_send()


def body(raw_echo, phase_scaling, phase_range, phase_azimuth):
    tiles = lax.axis_size("tile")
    length = lax.axis_size("az")
    rows_own = raw_echo.shape[1]
    pulses = rows_own * tiles
    extent, width = phase_scaling.shape
    count, ranges = phase_range.shape
    m, q, tail = extent // 4, pulses // 4, extent - pulses
    n_one, spans = ranges // LANES, width // LANES
    block = min(64, count)
    rows, lane = np.arange(m), np.arange(LANES)
    vmem = pl.BlockSpec(memory_space=pltpu.VMEM)
    anyspace = pl.BlockSpec(memory_space=pl.ANY)
    dma = pltpu.SemaphoreType.DMA
    spectrum = pl.pallas_call(
        functools.partial(front_kernel, tiles),
        out_shape=jax.ShapeDtypeStruct((2, extent, width), F32),
        in_specs=[anyspace, vmem, vmem, vmem],
        out_specs=vmem,
        scratch_shapes=[
            pltpu.VMEM((spans, 2, pulses, LANES), F32),
            dma((spans, tiles - 1)),
            dma((spans, tiles - 1)),
            dma((spans,)),
        ],
        compiler_params=pltpu.CompilerParams(
            collective_id=0, has_side_effects=True, vmem_limit_bytes=60 << 20
        ),
    )(
        raw_echo,
        left_table(rows, np.arange(q), m, -1),
        twist_table(4, m, extent, -1),
        phase_scaling,
    )
    turn = phase_range.reshape(count, LANES, n_one).transpose(2, 0, 1)
    c, s = roots(np.arange(n_one), lane, ranges, -1)
    return pl.pallas_call(
        functools.partial(back_kernel, tiles, length, block),
        out_shape=jax.ShapeDtypeStruct((2, pulses, width), F32),
        in_specs=[anyspace] + [vmem] * 7,
        out_specs=vmem,
        scratch_shapes=[
            pltpu.VMEM((2, count, ranges), F32),
            pltpu.VMEM((spans, 2, extent, LANES), F32),
            pltpu.VMEM((spans, 2, tail, LANES), F32),
            pltpu.VMEM((spans, 2, tail, LANES), F32),
            pltpu.VMEM((2, pulses, LANES), F32),
            pltpu.VMEM((n_one, block, 2 * LANES), BF16),
            pltpu.VMEM((n_one, block, 2 * LANES), BF16),
            pltpu.VMEM((n_one, block, 2 * LANES), F32),
            dma((count // block, tiles - 1)),
            dma((count // block, tiles - 1)),
            dma,
            dma((spans, tiles - 1)),
            dma((spans, tiles - 1)),
            dma((spans,)),
            dma((spans,)),
            dma((spans,)),
        ],
        compiler_params=pltpu.CompilerParams(
            collective_id=1, has_side_effects=True, vmem_limit_bytes=60 << 20
        ),
    )(
        spectrum,
        turn,
        phase_azimuth,
        right_table(lane, lane, LANES, -1),
        right_table(lane, lane, LANES, 1, 1.0 / ranges),
        np.stack([c, s]).astype(np.float32),
        left_table(rows, rows, m, 1, 1.0 / extent),
        twist_table(4, m, extent, 1),
    )


def solution(mesh):
    return jax.shard_map(
        body,
        mesh=mesh,
        in_specs=(
            P(None, ("strip", "az", "tile"), None),
            P(None, "tile"),
            P("tile", None),
            P(None, "tile"),
        ),
        out_specs=P(None, ("strip", "az"), "tile"),
        check_vma=False,
    )
```

time: 485 us -> 284 us (0.59)
  waiting for transfers between devices: 245 us -> 0 us
  Pallas kernels: 69.9 us -> 265 us
  local copies, waits for them, and re-layouts: 143 us -> 15.7 us
  starting transfers between devices: 21.1 us -> 0 us
    pallas_call x4 -> x2, Pallas kernels: 69.9 us -> 265 us  [the longest x1 210 us: body(): pl.pallas_call(functools.partial(back_kernel, tiles, length, block), out_...]
    all_to_all x3 -> x0, waiting for transfers between devices: 169 us -> none  [the longest x1 76.3 us: body(): lax.all_to_all(filtered[:, None], 'tile', split_axis=3, concat_axis=1, ti...]
    ppermute x1 -> x0, waiting for transfers between devices: 76.7 us -> none  [body(): incoming = lax.ppermute(rest, 'az', [(i, i + 1) for i in range(length - 1)])]
    sin x4 -> x0, local copies, waits for them, and re-layouts: 55.2 us -> none  [the longest x2 22 us: body(): jnp.sin(permuted)]
    all_to_all x3 -> x0, local copies, waits for them, and re-layouts: 32.6 us -> none  [the longest x1 13.3 us: body(): lax.all_to_all(filtered[:, None], 'tile', split_axis=3, concat_axis=1, ti...]
    all_to_all x3 -> x0, starting transfers between devices: 16.6 us -> none  [the longest x1 5.87 us: body(): lax.all_to_all(grouped, 'tile', split_axis=1, concat_axis=3, tiled=True)]
    reshape x2 -> x1, local copies, waits for them, and re-layouts: 19.2 us -> 5.31 us  [body(): turn = phase_range.reshape(count, LANES, n_one).transpose(2, 0, 1)]
    broadcast_in_dim x1 -> x0, local copies, waits for them, and re-layouts: 13.2 us -> none  [body(): filtered[:, None]]
  transfers between devices with their start and end apart: 4 -> 0, of which waited for: 4 -> 0; matrix products, arithmetic and copies ran while one was open for 14% -> 0% of each run, Pallas kernels for 3% -> 0%
where the time goes in v2:
time: 284 us; the launch traced here: 281 us
  Pallas kernels  265 us (93%)
  local copies, waits for them, and re-layouts  15.7 us (6%)
    pallas_call x1, Pallas kernels, body(): pl.pallas_call(functools.partial(back_kernel, tiles, length, block), out_...  210 us
    pallas_call x1, Pallas kernels, body(): pl.pallas_call(functools.partial(front_kernel, tiles), out_shape=jax.Shap...  55.2 us
    unnamed x2, local copies, waits for them, and re-layouts  10.4 us

profile of v2, /device:TPU:0, one launch (start us, length us, event | category | flops | bytes accessed | tf_op | source)
XLA Modules:
  0.0 280.7 jit_solution(9385356050378679034)
XLA Ops:
  0.0 5.6 %copy.12 = f32[256,4096]{0,1:T(8,128)} copy(f32[256,4096]{1,0:T(8,128)} %param.13) | data formatting | bytes 8388608 | tf_op args[2]
  5.6 5.3 %copy.13 = f32[256,128,32]{1,0,2:T(8,128)} copy(f32[256,128,32]{0,2,1:T(8,128)} %bitcast.2) | data formatting | bytes 8388608 | tf_op jit(solution)/shard_map/reshape | solution.py:420
  10.9 55.2 %shard_map.109.spec_ref = f32[2,1024,1024]{2,1,0:T(8,128)} custom-call(f32[2,128,4096]{2,1,0:T(8,128)} %raw_ref.1, bf16[2,512,256]{2,1,0:T(8,128)(2,1)} %constant.14.clone.table_ref, f32[2,4,256,128]{3,2,1,0:T(8,128)} %constant.15.clone.twist_ref, f32[1024,1024]{1,0:T(8,128)} %phase_ref.2), custom_call_target="tpu_custom_call" | custom-call | tf_op jit(solution)/shard_map/pallas_call | solution.py:400
  66.1 209.8 %shard_map.110 = f32[2,512,1024]{2,1,0:T(8,128)} custom-call(f32[2,1024,1024]{2,1,0:T(8,128)} %shard_map.109.spec_ref, f32[32,256,128]{2,1,0:T(8,128)} %bitcast.3, f32[1024,1024]{1,0:T(8,128)} %phase_ref.3, bf16[2,256,256]{2,1,0:T(8,128)(2,1)} %constant.16.clone.fwd_ref, bf16[2,256,256]{2,1,0:T(8,128)(2,1)} %constant.17.clone.inv_ref, ...), custom_call_target="tpu_custom_call" | custom-call | tf_op jit(solution)/shard_map/pallas_call | solution.py:422
  275.9 4.8 %copy.15 = f32[2,512,1024]{2,1,0:T(8,128)} copy(f32[2,512,1024]{2,1,0:T(8,128)} %shard_map.110) | data formatting | bytes 8388608

commit v3 on v2

v3 whole, which is shorter than its diff:
```python
import functools
import math

import jax
import jax.numpy as jnp
import numpy as np
from jax import lax
from jax.experimental import pallas as pl
from jax.experimental.pallas import tpu as pltpu
from jax.sharding import PartitionSpec as P

F32 = jnp.float32
BF16 = jnp.bfloat16
LANES = 128


def halves(table):
    hi = np.asarray(table, np.float32).astype(jnp.bfloat16)
    lo = (np.asarray(table, np.float64) - hi.astype(np.float64)).astype(jnp.bfloat16)
    return np.stack([hi, lo])


def roots(rows, cols, modulus, direction):
    residue = np.outer(rows, cols) % modulus
    angle = residue * (direction * 2.0 * math.pi / modulus)
    return np.cos(angle), np.sin(angle)


def left_table(rows, cols, modulus, direction, scale=1.0):
    c, s = roots(rows, cols, modulus, direction)
    return halves(np.block([[c, -s], [s, c]]) * scale)


def right_table(rows, cols, modulus, direction, scale=1.0):
    c, s = roots(rows, cols, modulus, direction)
    return halves(np.block([[c, s], [-s, c]]) * scale)


def twist_table(count, length, modulus, direction):
    c, s = roots(np.arange(count), np.arange(length), modulus, direction)
    full = np.stack([c, s]).astype(np.float32)
    return np.ascontiguousarray(np.broadcast_to(full[..., None], full.shape + (LANES,)))


def split(x):
    hi = x.astype(BF16)
    return hi, (x - hi.astype(F32)).astype(BF16)


def mm(a, b):
    return jnp.dot(a, b, preferred_element_type=F32)


def times(a, t):
    return a[0] * t[0] - a[1] * t[1], a[0] * t[1] + a[1] * t[0]


def plus(a, b):
    return a[0] + b[0], a[1] + b[1]


def minus(a, b):
    return a[0] - b[0], a[1] - b[1]


def quarter(a, direction):
    return (-a[1], a[0]) if direction > 0 else (a[1], -a[0])


def four(v, direction):
    a, b = plus(v[0], v[2]), minus(v[0], v[2])
    c, d = plus(v[1], v[3]), quarter(minus(v[1], v[3]), direction)
    return [plus(a, c), plus(b, d), minus(a, c), minus(b, d)]


def fft(v, direction):
    n = len(v)
    if n == 1:
        return v
    if n == 2:
        return [plus(v[0], v[1]), minus(v[0], v[1])]
    if n == 4:
        return four(v, direction)
    parts = [fft(v[e::4], direction) for e in range(4)] if n % 4 == 0 else None
    out = [None] * n
    m = n // 4
    for f in range(m):
        items = []
        for e in range(4):
            x = parts[e][f]
            k = e * f % n
            if k == 0:
                pass
            elif 8 * k == n:
                h = np.float32(math.sqrt(0.5))
                q = quarter(x, direction)
                x = ((x[0] + q[0]) * h, (x[1] + q[1]) * h)
            elif 4 * k == n:
                x = quarter(x, direction)
            elif 8 * k == 3 * n:
                h = np.float32(math.sqrt(0.5))
                q = quarter(x, direction)
                x = ((q[0] - x[0]) * h, (q[1] - x[1]) * h)
            else:
                ang = direction * 2.0 * math.pi * k / n
                x = times(x, (np.float32(math.cos(ang)), np.float32(math.sin(ang))))
            items.append(x)
        got = four(items, direction)
        for j in range(4):
            out[f + j * m] = got[j]
    return out


def sincos(x):
    y = x * 0.5
    z = y * y
    s, c = -1.0 / 39916800, 1.0 / 479001600
    for a, b in ((362880, -3628800), (-5040, 40320), (120, -720), (-6, 24), (1, -2)):
        s = s * z + np.float32(1.0 / a)
        c = c * z + np.float32(1.0 / b)
    s = s * y
    c = c * z + 1.0
    return 1.0 - 2.0 * s * s, 2.0 * s * c


def greet(partners):
    barrier = pltpu.get_barrier_semaphore()
    for device in partners:
        pl.semaphore_signal(barrier, inc=1, device_id=device, device_id_type=pl.DeviceIdType.MESH)
    return barrier


def lanes(j):
    return pl.ds(pl.multiple_of(j * LANES, LANES), LANES)


def filter_rows(x_ref, base, block, fwd_ref, inv_ref, twist_ref, phase_ref, hi_ref, lo_ref, mid_ref):
    n_one = phase_ref.shape[0]
    step = 16
    f_hi, f_lo = fwd_ref[0], fwd_ref[1]
    b_hi, b_lo = inv_ref[0], inv_ref[1]

    @pl.loop(0, block // step)
    def _(i):
        rows = pl.ds(pl.multiple_of(i * step, step), step)
        at = pl.ds(pl.multiple_of(base + i * step, step), step)
        v = [
            tuple(x_ref[c, at, pl.ds(a * LANES, LANES)] for c in (0, 1))
            for a in range(n_one)
        ]
        for k, x in enumerate(fft(v, -1)):
            if k:
                x = times(x, (twist_ref[0, k : k + 1, :], twist_ref[1, k : k + 1, :]))
            for c in (0, 1):
                h, l = split(x[c])
                hi_ref[k, rows, pl.ds(c * LANES, LANES)] = h
                lo_ref[k, rows, pl.ds(c * LANES, LANES)] = l

    group = 4

    @pl.loop(0, n_one // group)
    def _(i):
        ks = pl.ds(i * group, group)
        flat = (group * block, 2 * LANES)
        h, l = hi_ref[ks].reshape(flat), lo_ref[ks].reshape(flat)
        r = mm(h, f_hi) + mm(l, f_hi) + mm(h, f_lo)
        turn = phase_ref[ks, pl.ds(pl.multiple_of(base, block), block), :]
        r = times((r[:, :LANES], r[:, LANES:]), sincos(turn.reshape(group * block, LANES)))
        h, l = split(jnp.concatenate(r, axis=1))
        r = mm(h, b_hi) + mm(l, b_hi) + mm(h, b_lo)
        at = pl.ds(pl.multiple_of(i * group * block, block), group * block)
        mid_ref[0, at, :] = r[:, :LANES]
        mid_ref[1, at, :] = r[:, LANES:]

    @pl.loop(0, block // 8)
    def _(i):
        at = pl.ds(pl.multiple_of(base + i * 8, 8), 8)
        v = []
        for k in range(n_one):
            x = tuple(mid_ref[c, pl.ds(pl.multiple_of(k * block + i * 8, 8), 8), :] for c in (0, 1))
            if k:
                x = times(x, (twist_ref[0, k : k + 1, :], -twist_ref[1, k : k + 1, :]))
            v.append(x)
        for a, x in enumerate(fft(v, 1)):
            for c in (0, 1):
                x_ref[c, at, pl.ds(a * LANES, LANES)] = x[c]


def permute_turn(o_ref, mid, turn):
    n_one, count, _ = turn.shape
    half = mid.shape[1]
    some = min(count, LANES)
    part = half // n_one

    @pl.loop(0, count // some)
    def _(i):
        @pl.loop(0, n_one)
        def _(g):
            c, row, j = piece(g, count, o_ref)
            at = pl.ds(pl.multiple_of(row + i * some, some), some)
            x = o_ref[c, at, lanes(j)]
            if some < LANES:
                x = jnp.concatenate([x] * (LANES // some), axis=0)
            per = half // LANES
            mid[g // per, pl.ds(pl.multiple_of(g % per * LANES, LANES), LANES), :] = x.T

        @pl.loop(0, n_one)
        def _(k):
            rows = pl.ds(k, part, stride=n_one)
            x = jnp.concatenate([mid[h, rows, :] for h in range(LANES // part)], axis=0)
            at = pl.ds(pl.multiple_of(i * some, some), some)
            turn[k, at, :] = x.T[:some]


def piece(g, count, o_ref):
    across = o_ref.shape[2] // LANES
    down = o_ref.shape[1] // count
    return g // (across * down), g // across % down * count, g % across


def focus_kernel(
    tiles, length, block,
    raw_ref, scaling_ref, range_ref, azimuth_ref,
    front_ref, twist_ref, fwd_ref, inv_ref, range_twist_ref, table_ref,
    o_ref,
    spec, scaling, turn, phase, dop, ret, tail_out, tail_in, head, hi_ref, lo_ref, mid,
    send_e, recv_e, local_e, send_a, recv_a, local_a, send_b, recv_b, local_b,
    send_c, recv_c, load, load_range,
):
    me = lax.axis_index("tile")
    az = lax.axis_index("az")
    count = dop.shape[1]
    width = o_ref.shape[2]
    pulses = o_ref.shape[1]
    tail = tail_in.shape[2]
    rows_own = raw_ref.shape[1]
    n_one = turn.shape[0]
    blocks = count // block
    early = (blocks - 1) * block
    spans = width // LANES
    cols = tail_out
    m = spec.shape[1] // 4
    q = pulses // 4
    mine = pl.ds(pl.multiple_of(me * width, LANES), width)
    own = pl.ds(pl.multiple_of(me * count, count), count)
    own_pulses = pl.ds(pl.multiple_of(me * rows_own, rows_own), rows_own)

    def remote(src, dst, send, recv, device):
        return pltpu.make_async_remote_copy(
            src_ref=src, dst_ref=dst, send_sem=send, recv_sem=recv,
            device_id=device, device_id_type=pl.DeviceIdType.MESH,
        )

    def echo(j, k):
        to = lax.rem(me + k, tiles)
        return remote(
            raw_ref.at[:, :, lanes(to * spans + j)], cols.at[j, :, own_pulses, :],
            send_e.at[j, k - 1], recv_e.at[j, k - 1], {"tile": to},
        )

    def keep_echo(j):
        return pltpu.make_async_copy(
            raw_ref.at[:, :, lanes(me * spans + j)], cols.at[j, :, own_pulses, :], local_e.at[j]
        )

    def load_piece(g):
        c, row, j = piece(g, count, o_ref)
        return pltpu.make_async_copy(
            range_ref.at[:, lanes(g)],
            o_ref.at[c, pl.ds(pl.multiple_of(row, count), count), lanes(j)],
            load_range.at[g],
        )

    def out(i, k):
        to = lax.rem(me + k, tiles)
        return remote(
            spec.at[:, pl.ds(pl.multiple_of(to * count + i * block, block), block), :],
            dop.at[:, pl.ds(pl.multiple_of(i * block, block), block), mine],
            send_a.at[i, k - 1], recv_a.at[i, k - 1], {"tile": to},
        )

    def back_rows(j, k, lo, n, slot):
        to = lax.rem(me + k, tiles)
        return remote(
            dop.at[:, pl.ds(lo, n), lanes(to * spans + j)],
            ret.at[j, :, pl.ds(pl.multiple_of(me * count + lo, 8), n), :],
            send_b.at[slot, k - 1], recv_b.at[slot, k - 1], {"tile": to},
        )

    def first_rows(k):
        return back_rows(0, k, 0, early, spans)

    def last_rows(k):
        return back_rows(0, k, early, count - early, 0)

    def back(j, k):
        return back_rows(j, k, 0, count, j)

    def keep(j):
        return pltpu.make_async_copy(
            dop.at[:, :, lanes(me * spans + j)], ret.at[j, :, own, :], local_b.at[j]
        )

    def onward(j):
        return remote(
            tail_out.at[j], tail_in.at[j], send_c.at[j], recv_c.at[j],
            {"az": lax.rem(az + 1, length)},
        )

    barrier = greet(
        [{"tile": lax.rem(me + k, tiles)} for k in range(1, tiles)]
        + [{"az": lax.rem(az + 1, length)}, {"az": lax.rem(az + length - 1, length)}]
    )
    get_scaling = pltpu.make_async_copy(scaling_ref, scaling, load.at[0])
    get_phase = pltpu.make_async_copy(azimuth_ref, phase, load.at[1])
    pl.semaphore_wait(barrier, tiles + 1)

    @pl.loop(0, spans)
    def _(j):
        for k in range(1, tiles):
            echo(j, k).start()
        keep_echo(j).start()

    @pl.loop(0, n_one)
    def _(g):
        load_piece(g).start()

    get_scaling.start()
    get_phase.start()

    @pl.loop(0, n_one)
    def _(g):
        load_piece(g).wait()

    permute_turn(o_ref, mid, turn)
    get_scaling.wait()

    @pl.loop(0, spans)
    def _(j):
        for k in range(1, tiles):
            echo(j, k).wait_recv()
        keep_echo(j).wait()
        hi, lo = front_ref[0], front_ref[1]
        z = []
        for e in range(4):
            rows = pl.ds(e, q, stride=4)
            s = jnp.concatenate([cols[j, 0, rows, :], cols[j, 1, rows, :]], axis=0)
            s_hi, s_lo = split(s)
            r = mm(hi, s_hi) + mm(hi, s_lo) + mm(lo, s_hi)
            r = (r[:m], r[m:])
            if e:
                r = times(r, (twist_ref[0, e], -twist_ref[1, e]))
            z.append(r)
        for f, x in enumerate(four(z, -1)):
            rows = pl.ds(f * m, m)
            x = times(x, sincos(scaling[rows, lanes(j)]))
            spec[0, rows, lanes(j)] = x[0]
            spec[1, rows, lanes(j)] = x[1]

    @pl.loop(0, blocks)
    def _(i):
        for k in range(1, tiles):
            out(i, k).start()

    first = pltpu.make_async_copy(spec.at[:, own, :], dop.at[:, :, mine], local_a)
    first.start()
    first.wait()

    @pl.loop(0, blocks)
    def _(i):
        if early:
            @pl.when(i == blocks - 1)
            def _():
                for k in range(1, tiles):
                    first_rows(k).start()

        for k in range(1, tiles):
            out(i, k).wait_recv()
        filter_rows(
            dop, i * block, block, fwd_ref, inv_ref, range_twist_ref, turn,
            hi_ref, lo_ref, mid,
        )

    for k in range(1, tiles):
        last_rows(k).start()
    keep(0).start()

    @pl.loop(1, spans)
    def _(j):
        for k in range(1, tiles):
            back(j, k).start()
        keep(j).start()

    get_phase.wait()

    @pl.loop(0, spans)
    def _(j):
        @pl.when(j == 0)
        def _():
            for k in range(1, tiles):
                if early:
                    first_rows(k).wait_recv()
                last_rows(k).wait_recv()

        @pl.when(j > 0)
        def _():
            for k in range(1, tiles):
                back(j, k).wait_recv()

        keep(j).wait()
        hi, lo = table_ref[0], table_ref[1]
        v = []
        for f in range(4):
            rows = pl.ds(f * m, m)
            v.append(times((ret[j, 0, rows, :], ret[j, 1, rows, :]), sincos(phase[rows, lanes(j)])))
        for e, x in enumerate(four(v, 1)):
            if e:
                x = times(x, (twist_ref[0, e], twist_ref[1, e]))
            s_hi, s_lo = split(jnp.concatenate(x, axis=0))
            r = mm(hi, s_hi) + mm(hi, s_lo) + mm(lo, s_hi)
            for c in (0, 1):
                head[c, pl.ds(e, q, stride=4), :] = r[c * m : c * m + q]
                tail_out[j, c, pl.ds(e, m - q, stride=4), :] = r[c * m + q : (c + 1) * m]

        @pl.when(az < length - 1)
        def _():
            onward(j).start()

        o_ref[:, :, lanes(j)] = head[...]

    @pl.when(az > 0)
    def _():
        @pl.loop(0, spans)
        def _(j):
            onward(j).wait_recv()
            o_ref[:, pl.ds(0, tail), lanes(j)] += tail_in[j]

    @pl.loop(0, blocks)
    def _(i):
        for k in range(1, tiles):
            out(i, k).wait_send()

    for k in range(1, tiles):
        if early:
            first_rows(k).wait_send()
        last_rows(k).wait_send()

    @pl.loop(1, spans)
    def _(j):
        for k in range(1, tiles):
            back(j, k).wait_send()

    @pl.loop(0, spans)
    def _(j):
        for k in range(1, tiles):
            echo(j, k).wait_send()

    @pl.when(az < length - 1)
    def _():
        @pl.loop(0, spans)
        def _(j):
            onward(j).wait_send()


def body(raw_echo, phase_scaling, phase_range, phase_azimuth):
    tiles = lax.axis_size("tile")
    length = lax.axis_size("az")
    pulses = raw_echo.shape[1] * tiles
    extent, width = phase_scaling.shape
    count, ranges = phase_range.shape
    m, q, tail = extent // 4, pulses // 4, extent - pulses
    n_one, spans = ranges // LANES, width // LANES
    block = min(64, count)
    rows, lane = np.arange(m), np.arange(LANES)
    vmem = pl.BlockSpec(memory_space=pltpu.VMEM)
    anyspace = pl.BlockSpec(memory_space=pl.ANY)
    dma = pltpu.SemaphoreType.DMA
    c, s = roots(np.arange(n_one), lane, ranges, -1)
    return pl.pallas_call(
        functools.partial(focus_kernel, tiles, length, block),
        out_shape=jax.ShapeDtypeStruct((2, pulses, width), F32),
        in_specs=[anyspace] * 4 + [vmem] * 6,
        out_specs=vmem,
        scratch_shapes=[
            pltpu.VMEM((2, extent, width), F32),
            pltpu.VMEM((extent, width), F32),
            pltpu.VMEM((n_one, count, LANES), F32),
            pltpu.VMEM((extent, width), F32),
            pltpu.VMEM((2, count, ranges), F32),
            pltpu.VMEM((spans, 2, extent, LANES), F32),
            pltpu.VMEM((spans, 2, max(tail, pulses), LANES), F32),
            pltpu.VMEM((spans, 2, tail, LANES), F32),
            pltpu.VMEM((2, pulses, LANES), F32),
            pltpu.VMEM((n_one, block, 2 * LANES), BF16),
            pltpu.VMEM((n_one, block, 2 * LANES), BF16),
            pltpu.VMEM((2, n_one * block, LANES), F32),
            dma((spans, tiles - 1)),
            dma((spans, tiles - 1)),
            dma((spans,)),
            dma((count // block, tiles - 1)),
            dma((count // block, tiles - 1)),
            dma,
            dma((spans + 1, tiles - 1)),
            dma((spans + 1, tiles - 1)),
            dma((spans,)),
            dma((spans,)),
            dma((spans,)),
            dma((2,)),
            dma((n_one,)),
        ],
        compiler_params=pltpu.CompilerParams(
            collective_id=0, has_side_effects=True, vmem_limit_bytes=63 << 20
        ),
    )(
        raw_echo,
        phase_scaling,
        phase_range,
        phase_azimuth,
        left_table(rows, np.arange(q), m, -1),
        twist_table(4, m, extent, 1),
        right_table(lane, lane, LANES, -1),
        right_table(lane, lane, LANES, 1, 1.0 / ranges),
        np.stack([c, s]).astype(np.float32),
        left_table(rows, rows, m, 1, 1.0 / extent),
    )


def solution(mesh):
    return jax.shard_map(
        body,
        mesh=mesh,
        in_specs=(
            P(None, ("strip", "az", "tile"), None),
            P(None, "tile"),
            P("tile", None),
            P(None, "tile"),
        ),
        out_specs=P(None, ("strip", "az"), "tile"),
        check_vma=False,
    )
```

time: 284 us -> 260 us (0.915)
  Pallas kernels: 265 us -> 254 us
  local copies, waits for them, and re-layouts: 15.7 us -> 4.79 us
    pallas_call x2 -> x1, Pallas kernels: 265 us -> 254 us  [body(): pl.pallas_call(functools.partial(focus_kernel, tiles, length, block), out...]
    unnamed x2 -> x1, local copies, waits for them, and re-layouts: 10.4 us -> 4.79 us
    reshape x1 -> x0, local copies, waits for them, and re-layouts: 5.31 us -> none  [body(): turn = phase_range.reshape(count, LANES, n_one).transpose(2, 0, 1)]
where the time goes in v3:
time: 260 us; the launch traced here: 259 us
  Pallas kernels  254 us (98%)
  local copies, waits for them, and re-layouts  4.79 us (2%)
    pallas_call x1, Pallas kernels, body(): pl.pallas_call(functools.partial(focus_kernel, tiles, length, block), out...  254 us

profile of v3, /device:TPU:0, one launch (start us, length us, event | category | flops | bytes accessed | tf_op | source)
XLA Modules:
  0.0 259.0 jit_solution(9742450423413756013)
XLA Ops:
  0.0 254.2 %shard_map.100 = f32[2,512,1024]{2,1,0:T(8,128)} custom-call(f32[2,128,4096]{2,1,0:T(8,128)} %raw_ref.1, f32[1024,1024]{1,0:T(8,128)} %scaling_ref.1, f32[256,4096]{1,0:T(8,128)} %range_ref.1, f32[1024,1024]{1,0:T(8,128)} %azimuth_ref.1, bf16[2,512,256]{2,1,0:T(8,128)(2,1)} %constant.12.clone.front_ref, f32[2,4,256,128]{3,2,1,0:T(8,128)} %constant.13.clone.twist_ref, ...), custom_call_target="tpu_custom_call" | custom-call | tf_op jit(solution)/shard_map/pallas_call | solution.py:479
  254.2 4.8 %copy.12 = f32[2,512,1024]{2,1,0:T(8,128)} copy(f32[2,512,1024]{2,1,0:T(8,128)} %shard_map.100) | data formatting | bytes 8388608

commit v4 on v3

--- a/solution.py
+++ b/solution.py
@@ -222,8 +222,8 @@
     tiles, length, block,
     raw_ref, scaling_ref, range_ref, azimuth_ref,
     front_ref, twist_ref, fwd_ref, inv_ref, range_twist_ref, table_ref,
-    o_ref,
-    spec, scaling, turn, phase, dop, ret, tail_out, tail_in, head, hi_ref, lo_ref, mid,
+    o_ref, tail_in,
+    spec, scaling, turn, phase, dop, ret, tail_out, head, hi_ref, lo_ref, mid,
     send_e, recv_e, local_e, send_a, recv_a, local_a, send_b, recv_b, local_b,
     send_c, recv_c, load, load_range,
 ):
@@ -232,7 +232,7 @@
     count = dop.shape[1]
     width = o_ref.shape[2]
     pulses = o_ref.shape[1]
-    tail = tail_in.shape[2]
+    tail = tail_in.shape[1]
     rows_own = raw_ref.shape[1]
     n_one = turn.shape[0]
     blocks = count // block
@@ -271,13 +271,23 @@
             load_range.at[g],
         )
 
+    def out_part(i, k, lo, n, slot):
+        to = lax.rem(me + k, tiles)
+        at = pl.ds(pl.multiple_of(me * width + lo, LANES), n)
+        return remote(
+            spec.at[:, pl.ds(pl.multiple_of(to * count + i * block, block), block), pl.ds(lo, n)],
+            dop.at[:, pl.ds(pl.multiple_of(i * block, block), block), at],
+            send_a.at[slot, k - 1], recv_a.at[slot, k - 1], {"tile": to},
+        )
+
     def out(i, k):
-        to = lax.rem(me + k, tiles)
-        return remote(
-            spec.at[:, pl.ds(pl.multiple_of(to * count + i * block, block), block), :],
-            dop.at[:, pl.ds(pl.multiple_of(i * block, block), block), mine],
-            send_a.at[i, k - 1], recv_a.at[i, k - 1], {"tile": to},
-        )
+        return out_part(i, k, 0, width, i)
+
+    def first_out(k):
+        return out_part(0, k, 0, width - LANES, blocks)
+
+    def last_out(k):
+        return out_part(0, k, width - LANES, LANES, 0)
 
     def back_rows(j, k, lo, n, slot):
         to = lax.rem(me + k, tiles)
@@ -303,7 +313,7 @@
 
     def onward(j):
         return remote(
-            tail_out.at[j], tail_in.at[j], send_c.at[j], recv_c.at[j],
+            tail_out.at[j, :, pl.ds(0, tail), :], tail_in.at[:, :, lanes(j)], send_c.at[j], recv_c.at[j],
             {"az": lax.rem(az + 1, length)},
         )
 
@@ -337,6 +347,11 @@
 
     @pl.loop(0, spans)
     def _(j):
+        @pl.when(j == spans - 1)
+        def _():
+            for k in range(1, tiles):
+                first_out(k).start()
+
         for k in range(1, tiles):
             echo(j, k).wait_recv()
         keep_echo(j).wait()
@@ -357,7 +372,10 @@
             spec[0, rows, lanes(j)] = x[0]
             spec[1, rows, lanes(j)] = x[1]
 
-    @pl.loop(0, blocks)
+    for k in range(1, tiles):
+        last_out(k).start()
+
+    @pl.loop(1, blocks)
     def _(i):
         for k in range(1, tiles):
             out(i, k).start()
@@ -374,8 +392,17 @@
                 for k in range(1, tiles):
                     first_rows(k).start()
 
-        for k in range(1, tiles):
-            out(i, k).wait_recv()
+        @pl.when(i == 0)
+        def _():
+            for k in range(1, tiles):
+                first_out(k).wait_recv()
+                last_out(k).wait_recv()
+
+        @pl.when(i > 0)
+        def _():
+            for k in range(1, tiles):
+                out(i, k).wait_recv()
+
         filter_rows(
             dop, i * block, block, fwd_ref, inv_ref, range_twist_ref, turn,
             hi_ref, lo_ref, mid,
@@ -433,9 +460,12 @@
         @pl.loop(0, spans)
         def _(j):
             onward(j).wait_recv()
-            o_ref[:, pl.ds(0, tail), lanes(j)] += tail_in[j]
-
-    @pl.loop(0, blocks)
+
+    for k in range(1, tiles):
+        first_out(k).wait_send()
+        last_out(k).wait_send()
+
+    @pl.loop(1, blocks)
     def _(i):
         for k in range(1, tiles):
             out(i, k).wait_send()
@@ -476,11 +506,14 @@
     anyspace = pl.BlockSpec(memory_space=pl.ANY)
     dma = pltpu.SemaphoreType.DMA
     c, s = roots(np.arange(n_one), lane, ranges, -1)
-    return pl.pallas_call(
+    head, incoming = pl.pallas_call(
         functools.partial(focus_kernel, tiles, length, block),
-        out_shape=jax.ShapeDtypeStruct((2, pulses, width), F32),
+        out_shape=[
+            jax.ShapeDtypeStruct((2, pulses, width), F32),
+            jax.ShapeDtypeStruct((2, tail, width), F32),
+        ],
         in_specs=[anyspace] * 4 + [vmem] * 6,
-        out_specs=vmem,
+        out_specs=[vmem, anyspace],
         scratch_shapes=[
             pltpu.VMEM((2, extent, width), F32),
             pltpu.VMEM((extent, width), F32),
@@ -489,7 +522,6 @@
             pltpu.VMEM((2, count, ranges), F32),
             pltpu.VMEM((spans, 2, extent, LANES), F32),
             pltpu.VMEM((spans, 2, max(tail, pulses), LANES), F32),
-            pltpu.VMEM((spans, 2, tail, LANES), F32),
             pltpu.VMEM((2, pulses, LANES), F32),
             pltpu.VMEM((n_one, block, 2 * LANES), BF16),
             pltpu.VMEM((n_one, block, 2 * LANES), BF16),
@@ -497,8 +529,8 @@
             dma((spans, tiles - 1)),
             dma((spans, tiles - 1)),
             dma((spans,)),
-            dma((count // block, tiles - 1)),
-            dma((count // block, tiles - 1)),
+            dma((count // block + 1, tiles - 1)),
+            dma((count // block + 1, tiles - 1)),
             dma,
             dma((spans + 1, tiles - 1)),
             dma((spans + 1, tiles - 1)),
@@ -523,6 +555,10 @@
         np.stack([c, s]).astype(np.float32),
         left_table(rows, rows, m, 1, 1.0 / extent),
     )
+    joined = head[:, :tail] + incoming
+    if tail < pulses:
+        joined = jnp.concatenate([joined, head[:, tail:]], axis=1)
+    return jnp.where(lax.axis_index("az") > 0, joined, head)
 
 
 def solution(mesh):

time: 260 us -> 259 us (level)
  other arithmetic: 0 us -> 6.92 us
  local copies, waits for them, and re-layouts: 4.79 us -> 0 us
  Pallas kernels: 254 us -> 251 us
    select_n x0 -> x1, other arithmetic: none -> 6.92 us  [body(): return jnp.where(lax.axis_index('az') > 0, joined, head)]
    unnamed x1 -> x0, local copies, waits for them, and re-layouts: 4.79 us -> none
    pallas_call x1, Pallas kernels: 254 us -> 251 us  [body(): pl.pallas_call(functools.partial(focus_kernel, tiles, length, block), out...]
where the time goes in v4:
time: 259 us; the launch traced here: 258 us
  Pallas kernels  251 us (97%)
  other arithmetic  6.92 us (3%)
    pallas_call x1, Pallas kernels, body(): pl.pallas_call(functools.partial(focus_kernel, tiles, length, block), out...  251 us
    select_n x1, other arithmetic, body(): return jnp.where(lax.axis_index('az') > 0, joined, head)  6.92 us

profile of v4, /device:TPU:0, one launch (start us, length us, event | category | flops | bytes accessed | tf_op | source)
XLA Modules:
  0.0 257.8 jit_solution(17224584029067006136)
XLA Ops:
  0.0 250.9 %shard_map.100 = (f32[2,512,1024]{2,1,0:T(8,128)}, f32[2,512,1024]{2,1,0:T(8,128)}) custom-call(f32[2,128,4096]{2,1,0:T(8,128)} %raw_ref.1, f32[1024,1024]{1,0:T(8,128)} %scaling_ref.1, f32[256,4096]{1,0:T(8,128)} %range_ref.1, f32[1024,1024]{1,0:T(8,128)} %azimuth_ref.1, bf16[2,512,256]{2,1,0:T(8,128)(2,1)} %constant.19.clone.front_ref, ...), custom_call_target="tpu_custom_call" | custom-call | tf_op jit(solution)/shard_map/pallas_call | solution.py:509
  250.9 6.9 %add_select_fusion = f32[2,512,1024]{2,1,0:T(8,128)} fusion(f32[2,512,1024]{2,1,0:T(8,128)} %get-tuple-element.7, f32[2,512,1024]{2,1,0:T(8,128)} %get-tuple-element.8, pred[]{:T(512)S(6)} %gt.3), kind=kLoop, calls=%fused_computation | loop fusion | flops 2097152 | bytes 12582913 | tf_op jit(solution)/shard_map/jit(_where)/select_n | solution.py:561

commit v5 on v4

--- a/solution.py
+++ b/solution.py
@@ -222,8 +222,8 @@
     tiles, length, block,
     raw_ref, scaling_ref, range_ref, azimuth_ref,
     front_ref, twist_ref, fwd_ref, inv_ref, range_twist_ref, table_ref,
-    o_ref, tail_in,
-    spec, scaling, turn, phase, dop, ret, tail_out, head, hi_ref, lo_ref, mid,
+    o_ref,
+    spec, scaling, turn, phase, dop, ret, tail_out, tail_in, head, hi_ref, lo_ref, mid,
     send_e, recv_e, local_e, send_a, recv_a, local_a, send_b, recv_b, local_b,
     send_c, recv_c, load, load_range,
 ):
@@ -232,7 +232,7 @@
     count = dop.shape[1]
     width = o_ref.shape[2]
     pulses = o_ref.shape[1]
-    tail = tail_in.shape[1]
+    tail = tail_in.shape[2]
     rows_own = raw_ref.shape[1]
     n_one = turn.shape[0]
     blocks = count // block
@@ -313,7 +313,7 @@
 
     def onward(j):
         return remote(
-            tail_out.at[j, :, pl.ds(0, tail), :], tail_in.at[:, :, lanes(j)], send_c.at[j], recv_c.at[j],
+            tail_out.at[j, :, pl.ds(0, tail), :], tail_in.at[j], send_c.at[j], recv_c.at[j],
             {"az": lax.rem(az + 1, length)},
         )
 
@@ -338,11 +338,6 @@
     get_scaling.start()
     get_phase.start()
 
-    @pl.loop(0, n_one)
-    def _(g):
-        load_piece(g).wait()
-
-    permute_turn(o_ref, mid, turn)
     get_scaling.wait()
 
     @pl.loop(0, spans)
@@ -382,6 +377,12 @@
 
     first = pltpu.make_async_copy(spec.at[:, own, :], dop.at[:, :, mine], local_a)
     first.start()
+
+    @pl.loop(0, n_one)
+    def _(g):
+        load_piece(g).wait()
+
+    permute_turn(o_ref, mid, turn)
     first.wait()
 
     @pl.loop(0, blocks)
@@ -460,6 +461,7 @@
         @pl.loop(0, spans)
         def _(j):
             onward(j).wait_recv()
+            o_ref[:, pl.ds(0, tail), lanes(j)] += tail_in[j]
 
     for k in range(1, tiles):
         first_out(k).wait_send()
@@ -506,14 +508,11 @@
     anyspace = pl.BlockSpec(memory_space=pl.ANY)
     dma = pltpu.SemaphoreType.DMA
     c, s = roots(np.arange(n_one), lane, ranges, -1)
-    head, incoming = pl.pallas_call(
+    return pl.pallas_call(
         functools.partial(focus_kernel, tiles, length, block),
-        out_shape=[
-            jax.ShapeDtypeStruct((2, pulses, width), F32),
-            jax.ShapeDtypeStruct((2, tail, width), F32),
-        ],
+        out_shape=jax.ShapeDtypeStruct((2, pulses, width), F32),
         in_specs=[anyspace] * 4 + [vmem] * 6,
-        out_specs=[vmem, anyspace],
+        out_specs=vmem,
         scratch_shapes=[
             pltpu.VMEM((2, extent, width), F32),
             pltpu.VMEM((extent, width), F32),
@@ -522,6 +521,7 @@
             pltpu.VMEM((2, count, ranges), F32),
             pltpu.VMEM((spans, 2, extent, LANES), F32),
             pltpu.VMEM((spans, 2, max(tail, pulses), LANES), F32),
+            pltpu.VMEM((spans, 2, tail, LANES), F32),
             pltpu.VMEM((2, pulses, LANES), F32),
             pltpu.VMEM((n_one, block, 2 * LANES), BF16),
             pltpu.VMEM((n_one, block, 2 * LANES), BF16),
@@ -555,10 +555,6 @@
         np.stack([c, s]).astype(np.float32),
         left_table(rows, rows, m, 1, 1.0 / extent),
     )
-    joined = head[:, :tail] + incoming
-    if tail < pulses:
-        joined = jnp.concatenate([joined, head[:, tail:]], axis=1)
-    return jnp.where(lax.axis_index("az") > 0, joined, head)
 
 
 def solution(mesh):

time: 259 us -> 257 us (level)
  other arithmetic: 6.92 us -> 0 us
  local copies, waits for them, and re-layouts: 0 us -> 4.79 us
    select_n x1 -> x0, other arithmetic: 6.92 us -> none  [body(): return jnp.where(lax.axis_index('az') > 0, joined, head)]
    unnamed x0 -> x1, local copies, waits for them, and re-layouts: none -> 4.79 us
where the time goes in v5:
time: 257 us; the launch traced here: 256 us
  Pallas kernels  251 us (98%)
  local copies, waits for them, and re-layouts  4.79 us (2%)
    pallas_call x1, Pallas kernels, body(): pl.pallas_call(functools.partial(focus_kernel, tiles, length, block), out...  251 us

profile of v5, /device:TPU:0, one launch (start us, length us, event | category | flops | bytes accessed | tf_op | source)
XLA Modules:
  0.0 255.7 jit_solution(15574470003760717154)
XLA Ops:
  0.0 250.9 %shard_map.100 = f32[2,512,1024]{2,1,0:T(8,128)} custom-call(f32[2,128,4096]{2,1,0:T(8,128)} %raw_ref.1, f32[1024,1024]{1,0:T(8,128)} %scaling_ref.1, f32[256,4096]{1,0:T(8,128)} %range_ref.1, f32[1024,1024]{1,0:T(8,128)} %azimuth_ref.1, bf16[2,512,256]{2,1,0:T(8,128)(2,1)} %constant.12.clone.front_ref, f32[2,4,256,128]{3,2,1,0:T(8,128)} %constant.13.clone.twist_ref, ...), custom_call_target="tpu_custom_call" | custom-call | tf_op jit(solution)/shard_map/pallas_call | solution.py:511
  250.9 4.8 %copy.12 = f32[2,512,1024]{2,1,0:T(8,128)} copy(f32[2,512,1024]{2,1,0:T(8,128)} %shard_map.100) | data formatting | bytes 8388608
